TPU v7x, 512 devices: a whole 4x8x8 slice. The times are simulated.
512 devices in a mesh: ops: 8 (over x, core), sec: 64 (over y, z).
Axes of the slice: x: 4, y: 8, z: 8, core: 2. Of those that a mesh axis runs over, the one named last changes fastest.
Arguments:
- wavefunction: bfloat16 [64, 4, 512, 512], P('sec'), may hold values from -6 to 6
- left_ops: bfloat16 [8, 3, 64, 512, 512], P('ops', None, 'sec'), may hold values from -0.25 to 0.25
- right_ops: bfloat16 [8, 3, 64, 512, 512], P('ops', None, 'sec'), may hold values from -0.25 to 0.25
- size_left: int32 [64], P('sec'), may hold values from 64 to 512, as said below
- size_right: int32 [64], P('sec'), may hold values from 64 to 512, as said below
Outputs:
- sigma: bfloat16 [64, 4, 512, 512], P('sec', None, 'ops')
Inputs may be any that keep to these rules, and one draw needn't show every extreme that they name: `size_left`: sector sizes; some sector has exactly 512 states in every draw. `size_right`: sector sizes; some sector has exactly 512 states in every draw.
All inputs are finite; a program needn't handle non-finite values.
Results may differ from a plain program's by a relative error of at most 0.013.
Values may be sent and summed in bfloat16 or wider, within the bound.
No kernel may reach another device: no remote copies, remote signals or barrier semaphores. Data moves between devices by JAX's collectives and lax.ppermute only.
A program may use at most 64 MiB of HBM per device.

v0:
```python
import functools

import jax
import jax.numpy as jnp
from jax import lax
from jax.experimental import pallas as pl
from jax.experimental.pallas import tpu as pltpu
from jax.sharding import PartitionSpec as P


W = 4
LANE = 128


def shifted(shard, by):
    size = lax.axis_size("sec")
    return lax.ppermute(shard, "sec", [(i, (i + by) % size) for i in range(size)])


def lift_kernel(size_ref, left_ref, vector_ref, out_ref):
    vector = vector_ref[0, 0]
    rows = lax.broadcasted_iota(jnp.int32, vector.shape, 0)
    vector = jnp.where(rows < size_ref[0], vector, jnp.zeros_like(vector))
    for t in range(left_ref.shape[1]):
        out_ref[0, t] = jnp.dot(
            left_ref[0, t, 0], vector, preferred_element_type=jnp.float32
        ).astype(jnp.bfloat16)


def lift(left_ops, wavefunction, size_left):
    channels, width = wavefunction.shape[1], wavefunction.shape[-1]
    terms = left_ops.shape[1]
    return pl.pallas_call(
        lift_kernel,
        grid=(channels,),
        in_specs=[
            pl.BlockSpec(memory_space=pltpu.SMEM),
            pl.BlockSpec(left_ops.shape, lambda c: (0, 0, 0, 0, 0)),
            pl.BlockSpec((1, 1, width, width), lambda c: (0, c, 0, 0)),
        ],
        out_specs=pl.BlockSpec((1, terms, width, width), lambda c: (c, 0, 0, 0)),
        out_shape=jax.ShapeDtypeStruct((channels, terms, width, width), jnp.bfloat16),
        cost_estimate=pl.CostEstimate(
            flops=2 * channels * terms * width**3, bytes_accessed=10 * 2**20, transcendentals=0
        ),
        name="lift",
    )(size_left, left_ops, wavefunction)


def finish_kernel(jobs, *refs):
    out_ref = refs[-1]
    ops, _, rows, _ = out_ref.shape
    at = 0
    for lifted, parts, columns in jobs:
        total = None
        for piece, first, lane in parts:
            deep = refs[piece].shape[2]
            for t in range(refs[piece].shape[0]):
                term = lax.dot_general(
                    refs[lifted][0, t, :, lane : lane + deep],
                    refs[piece][t, first : first + columns, :],
                    (((1,), (1,)), ((), ())),
                    preferred_element_type=jnp.float32,
                )
                total = term if total is None else total + term
        total = total.astype(jnp.bfloat16)
        for block in range(columns // LANE):
            out_ref[:, at] = total[:, block * LANE : (block + 1) * LANE].reshape(ops, rows, LANE)
            at += 1


def finish(lifted, jobs):
    ops, width = lax.axis_size("ops"), lifted.shape[-1]
    channels = sorted({job[0] for job in jobs})
    arrays = [lifted] * len(channels)
    specs = [
        pl.BlockSpec((1, *lifted.shape[1:]), functools.partial(lambda c, i: (c, 0, 0, 0), c)) for c in channels
    ]
    place, table = {}, []
    for channel, parts, columns in jobs:
        row = []
        for piece, first, lane in parts:
            if id(piece) not in place:
                place[id(piece)] = len(arrays)
                arrays.append(piece)
                specs.append(pl.BlockSpec(piece.shape, lambda i: (0, 0, 0)))
            row.append((place[id(piece)], first, lane))
        table.append((channels.index(channel), row, columns))
    shape = (ops, sum(job[2] for job in jobs) // LANE, width // ops, LANE)
    columns = sum(job[2] for job in jobs)
    return pl.pallas_call(
        functools.partial(finish_kernel, table),
        grid=(1,),
        in_specs=specs,
        out_specs=pl.BlockSpec(shape, lambda i: (0, 0, 0, 0)),
        out_shape=jax.ShapeDtypeStruct(shape, jnp.bfloat16),
        cost_estimate=pl.CostEstimate(
            flops=2 * columns * width * width * lifted.shape[1],
            bytes_accessed=2 * 2**20 + columns * 3 * 2**10,
            transcendentals=0,
        ),
    )(*arrays)


def exchanged(part):
    return lax.all_to_all(part, "ops", 0, 0, tiled=True)


def summed(pieces):
    return jnp.sum(pieces.astype(jnp.float32), axis=0)


def body(wavefunction, left_ops, right_ops, size_left, size_right):
    offsets = (0, 1, W, W + 1)
    width = wavefunction.shape[-1]
    ops = lax.axis_size("ops")
    place = jnp.arange(width, dtype=jnp.int32)
    keep = place < size_right[0]

    def cut(r0, r1, c0, c1):
        inside = keep[r0:r1, None] & keep[None, c0:c1]
        return jnp.where(inside, right_ops[0, :, 0, r0:r1, c0:c1], jnp.zeros((), jnp.bfloat16))

    half, lane = width // 2, 3 * width // 4
    a0, a1 = cut(0, LANE, 0, lane), cut(LANE, half, 0, lane)
    b0, b1 = cut(half, width, 0, lane), cut(0, width, lane, width)
    a0_1 = shifted(a0, -1)
    b1_1 = shifted(b1, 1 - 2 * W)
    a1_1 = shifted(a1, -1)
    b0_1 = shifted(b0, 1 - 2 * W)
    n1 = shifted(b1, -1)
    a0_2 = shifted(a0_1, -1)
    a1_2 = shifted(a1_1, -1)
    b1_2 = shifted(b1_1, 1)
    n0 = shifted(b0, -1)
    b0_2 = shifted(b0_1, 1)
    a0_3 = shifted(a0_2, -1)
    b1_3 = shifted(b1_2, 1)
    a1_3 = shifted(a1_2, -1)
    b0_3 = shifted(b0_2, 1)
    a0_4 = shifted(a0_3, -1)
    b1_4 = shifted(b1_3, 1)
    a1_4 = shifted(a1_3, -1)
    b0_4 = shifted(b0_3, 1)
    a0_5 = shifted(a0_4, -1)
    a1_5 = shifted(a1_4, -1)

    lifted = lift(left_ops, wavefunction, size_left)

    def top0(a, b):
        return [(a, 0, 0), (b, 0, lane)], LANE

    def top1(a, b):
        return [(a, 0, 0), (b, LANE, lane)], LANE

    def low(b, c):
        return [(b, 0, 0), (c, half, lane)], half

    x0 = exchanged(finish(lifted, [(0, *top0(a0, b1)), (0, *top1(a1, b1)), (0, *low(b0, b1))]))
    x1 = exchanged(finish(lifted, [(1, *top0(a0_1, n1)), (1, *top1(a1_1, n1)), (1, *low(n0, n1))]))
    x2 = exchanged(finish(lifted, [(3, *low(b0_3, b1_3))]))
    x3 = exchanged(finish(lifted, [(2, *top0(a0_4, b1_4)), (2, *top1(a1_4, b1_4)), (3, *top0(a0_5, b1_3))]))
    x4 = exchanged(finish(lifted, [(2, *low(b0_4, b1_4)), (3, *top1(a1_5, b1_3))]))
    s0, s1, s2, s3, s4 = (summed(x) for x in (x0, x1, x2, x3, x4))
    blocks = [
        [s0[0], s0[1], s0[2], s0[3]],
        [s1[0], s1[1], s1[2], s1[3]],
        [s3[0], s3[1], s4[0], s4[1]],
        [s3[2], s4[2], s2[0], s2[1]],
    ]
    sums = jnp.stack([jnp.concatenate(row, axis=1) for row in blocks])
    rows = width // ops
    row_at = lax.axis_index("ops") * rows + jnp.arange(rows, dtype=jnp.int32)
    exists = lax.axis_index("sec") + jnp.array(offsets, jnp.int32) < lax.axis_size("sec")
    kept = (row_at < size_left[0])[None, :, None] & exists[:, None, None]
    return jnp.where(kept, sums, 0.0).astype(jnp.bfloat16)[None]


def solution(mesh):
    placed = (
        P("sec", None, None, None),
        P("ops", None, "sec", None, None),
        P("ops", None, "sec", None, None),
        P("sec"),
        P("sec"),
    )

    return jax.shard_map(body, mesh=mesh, in_specs=placed, out_specs=P("sec", None, "ops", None), check_vma=False)
```

profile of v0, /device:TPU:1, one launch (start us, length us, event | category | flops | bytes accessed | tf_op | source)
XLA Modules:
  0.0 183.8 jit_solution(493021082316709553)
XLA Ops:
  1.9 7.7 %collective-permute-start.7 = (bf16[3,512,128]{2,1,0:T(8,128)(2,1)S(1)}, bf16[3,512,128]{2,1,0:T(8,128)(2,1)S(1)}, u32[]{:S(2)}, u32[]{:S(2)}) collective-permute-start(bf16[3,512,128]{2,1,0:T(8,128)(2,1)S(1)} %fusion.2.refs_2_), channel_id=1, source_target_pairs={{0,57},{1,58},{2,59},{3,60},{4,61},{5,62},{6,63},{7,0},{8,1},{9,2}... | collective-permute-start | bytes 1179656 | tf_op jit(solution)/shard_map/ppermute | solution.py:17
  10.9 4.8 %collective-permute-start.15 = (bf16[3,256,384]{2,1,0:T(8,128)(2,1)S(1)}, bf16[3,256,384]{2,1,0:T(8,128)(2,1)}, u32[]{:S(2)}, u32[]{:S(2)}) collective-permute-start(bf16[3,256,384]{2,1,0:T(8,128)(2,1)S(1)} %fusion.refs_4_), channel_id=1, source_target_pairs={{0,57},{1,58},{2,59},{3,60},{4,61},{5,62},{6,63},{7,0},{8,1},{9,2}... | collective-permute-start | bytes 1769480 | tf_op jit(solution)/shard_map/ppermute | solution.py:17
  17.0 5.7 %collective-permute-start = (bf16[3,128,384]{2,1,0:T(8,128)(2,1)S(1)}, bf16[3,128,384]{2,1,0:T(8,128)(2,1)S(1)}, u32[]{:S(2)}, u32[]{:S(2)}) collective-permute-start(bf16[3,128,384]{2,1,0:T(8,128)(2,1)S(1)} %get-tuple-element.5.refs_1_), channel_id=1, source_target_pairs={{0,63},{1,0},{2,1},{3,2},{4,3},{5,4},{6,5},{7,6},{8,7},{9,8},{10,9... | collective-permute-start | bytes 884744 | tf_op jit(solution)/shard_map/ppermute | solution.py:17
  22.7 4.1 %collective-permute-start.2 = (bf16[3,128,384]{2,1,0:T(8,128)(2,1)S(1)}, bf16[3,128,384]{2,1,0:T(8,128)(2,1)S(1)}, u32[]{:S(2)}, u32[]{:S(2)}) collective-permute-start(bf16[3,128,384]{2,1,0:T(8,128)(2,1)S(1)} %get-tuple-element.6.refs_3_), channel_id=1, source_target_pairs={{0,63},{1,0},{2,1},{3,2},{4,3},{5,4},{6,5},{7,6},{8,7},{9,8},{10,9... | collective-permute-start | bytes 884744 | tf_op jit(solution)/shard_map/ppermute | solution.py:17
  26.9 4.1 %collective-permute-start.1 = (bf16[3,512,128]{2,1,0:T(8,128)(2,1)S(1)}, bf16[3,512,128]{2,1,0:T(8,128)(2,1)S(1)}, u32[]{:S(2)}, u32[]{:S(2)}) collective-permute-start(bf16[3,512,128]{2,1,0:T(8,128)(2,1)S(1)} %fusion.2.refs_2_), channel_id=1, source_target_pairs={{0,63},{1,0},{2,1},{3,2},{4,3},{5,4},{6,5},{7,6},{8,7},{9,8},{10,9... | collective-permute-start | bytes 1179656 | tf_op jit(solution)/shard_map/ppermute | solution.py:17
  31.7 4.6 %collective-permute-done.refs_1_ = bf16[3,128,384]{2,1,0:T(8,128)(2,1)S(1)} collective-permute-done((bf16[3,128,384]{2,1,0:T(8,128)(2,1)S(1)}, bf16[3,128,384]{2,1,0:T(8,128)(2,1)S(1)}, u32[]{:S(2)}, u32[]{:S(2)}) %collective-permute-start) | collective-permute-done | bytes 294944 | tf_op jit(solution)/shard_map/ppermute | solution.py:17
  36.3 7.4 %collective-permute-start.3 = (bf16[3,256,384]{2,1,0:T(8,128)(2,1)S(1)}, bf16[3,256,384]{2,1,0:T(8,128)(2,1)S(1)}, u32[]{:S(2)}, u32[]{:S(2)}) collective-permute-start(bf16[3,256,384]{2,1,0:T(8,128)(2,1)S(1)} %fusion.refs_4_), channel_id=1, source_target_pairs={{0,63},{1,0},{2,1},{3,2},{4,3},{5,4},{6,5},{7,6},{8,7},{9,8},{10,9... | collective-permute-start | bytes 1769480 | tf_op jit(solution)/shard_map/ppermute | solution.py:17
  43.7 6.3 %collective-permute-start.4 = (bf16[3,128,384]{2,1,0:T(8,128)(2,1)S(1)}, bf16[3,128,384]{2,1,0:T(8,128)(2,1)}, u32[]{:S(2)}, u32[]{:S(2)}) collective-permute-start(bf16[3,128,384]{2,1,0:T(8,128)(2,1)S(1)} %collective-permute-done.refs_1_), channel_id=1, source_target_pairs={{0,63},{1,0},{2,1},{3,2},{4,3},{5,4},{6,5},{7,6},{8,7},{9,8},{10,9... | collective-permute-start | bytes 884744 | tf_op jit(solution)/shard_map/ppermute | solution.py:17
  53.9 7.4 %lift.1.refs_0_.refs_1_ = bf16[4,3,512,512]{3,2,1,0:T(8,128)(2,1)} custom-call(s32[1]{0:T(128)} %copy.11.size_ref, bf16[1,3,1,512,512]{4,3,2,1,0:T(8,128)(2,1)} %left_ref.1, bf16[1,4,512,512]{3,2,1,0:T(8,128)(2,1)} %vector_ref.1), custom_call_target="tpu_custom_call" | custom-call | flops 3221225472 | bytes 10485760 | tf_op jit(solution)/shard_map/lift/pallas_call | solution.py:33
  61.4 4.3 %shard_map.64 = bf16[8,4,64,128]{3,2,1,0:T(8,128)(2,1)} custom-call(bf16[4,3,512,512]{3,2,1,0:T(8,128)(2,1)} %lift.1.refs_0_.refs_1_, bf16[3,128,384]{2,1,0:T(8,128)(2,1)} %copy-done.4, bf16[3,512,128]{2,1,0:T(8,128)(2,1)} %copy-done.2, bf16[3,128,384]{2,1,0:T(8,128)(2,1)} %copy-done.5, bf16[3,256,384]{2,1,0:T(8,128)(2,1)} %copy-done.1), custom_call_target="tpu_custom_call" | custom-call | flops 805306368 | bytes 3670016 | tf_op jit(solution)/shard_map/pallas_call | solution.py:91
  65.7 7.3 %all-to-all-start = ((bf16[8,4,64,128]{3,2,1,0:T(8,128)(2,1)}), bf16[8,4,64,128]{3,2,1,0:T(8,128)(2,1)S(1)}, u32[]{:S(2)}, u32[]{:S(2)}) async-start(bf16[8,4,64,128]{3,2,1,0:T(8,128)(2,1)} %shard_map.64), calls=%async_computation | async-start | bytes 1048576 | tf_op jit(solution)/shard_map/all_to_all | solution.py:106
  73.0 7.0 %collective-permute-start.11 = (bf16[3,128,384]{2,1,0:T(8,128)(2,1)S(1)}, bf16[3,128,384]{2,1,0:T(8,128)(2,1)}, u32[]{:S(2)}, u32[]{:S(2)}) collective-permute-start(bf16[3,128,384]{2,1,0:T(8,128)(2,1)S(1)} %collective-permute-done.2.refs_3_), channel_id=1, source_target_pairs={{0,63},{1,0},{2,1},{3,2},{4,3},{5,4},{6,5},{7,6},{8,7},{9,8},{10,9... | collective-permute-start | bytes 884744 | tf_op jit(solution)/shard_map/ppermute | solution.py:17
  86.3 7.5 %collective-permute-start.12 = (bf16[3,128,384]{2,1,0:T(8,128)(2,1)}, bf16[3,128,384]{2,1,0:T(8,128)(2,1)S(1)}, u32[]{:S(2)}, u32[]{:S(2)}) collective-permute-start(bf16[3,128,384]{2,1,0:T(8,128)(2,1)} %collective-permute-done.11), channel_id=1, source_target_pairs={{0,63},{1,0},{2,1},{3,2},{4,3},{5,4},{6,5},{7,6},{8,7},{9,8},{10,9... | collective-permute-start | bytes 884744 | tf_op jit(solution)/shard_map/ppermute | solution.py:17
  94.7 4.2 %shard_map.65 = bf16[8,4,64,128]{3,2,1,0:T(8,128)(2,1)} custom-call(bf16[4,3,512,512]{3,2,1,0:T(8,128)(2,1)} %lift.1.refs_0_.refs_1_, bf16[3,128,384]{2,1,0:T(8,128)(2,1)} %copy-done.10, bf16[3,512,128]{2,1,0:T(8,128)(2,1)} %copy-done.9, bf16[3,128,384]{2,1,0:T(8,128)(2,1)} %copy-done.11, bf16[3,256,384]{2,1,0:T(8,128)(2,1)} %copy-done.7), custom_call_target="tpu_custom_call" | custom-call | flops 805306368 | bytes 3670016 | tf_op jit(solution)/shard_map/pallas_call | solution.py:91
  104.3 7.0 %all-to-all-start.1 = ((bf16[8,4,64,128]{3,2,1,0:T(8,128)(2,1)}), bf16[8,4,64,128]{3,2,1,0:T(8,128)(2,1)S(1)}, u32[]{:S(2)}, u32[]{:S(2)}) async-start(bf16[8,4,64,128]{3,2,1,0:T(8,128)(2,1)} %shard_map.65), calls=%async_computation.1 | async-start | bytes 1048576 | tf_op jit(solution)/shard_map/all_to_all | solution.py:106
  113.3 6.7 %collective-permute-start.13 = (bf16[3,128,384]{2,1,0:T(8,128)(2,1)S(1)}, bf16[3,128,384]{2,1,0:T(8,128)(2,1)S(1)}, u32[]{:S(2)}, u32[]{:S(2)}) collective-permute-start(bf16[3,128,384]{2,1,0:T(8,128)(2,1)S(1)} %collective-permute-done.12), channel_id=1, source_target_pairs={{0,63},{1,0},{2,1},{3,2},{4,3},{5,4},{6,5},{7,6},{8,7},{9,8},{10,9... | collective-permute-start | bytes 884744 | tf_op jit(solution)/shard_map/ppermute | solution.py:17
  126.1 6.3 %collective-permute-done.14.refs_5_ = bf16[3,128,384]{2,1,0:T(8,128)(2,1)S(1)} collective-permute-done((bf16[3,128,384]{2,1,0:T(8,128)(2,1)S(1)}, bf16[3,128,384]{2,1,0:T(8,128)(2,1)S(1)}, u32[]{:S(2)}, u32[]{:S(2)}) %collective-permute-start.14) | collective-permute-done | bytes 294944 | tf_op jit(solution)/shard_map/ppermute | solution.py:17
  133.9 4.5 %shard_map.66 = bf16[8,3,64,128]{3,2,1,0:T(8,128)(2,1)} custom-call(bf16[4,3,512,512]{3,2,1,0:T(8,128)(2,1)} %lift.1.refs_0_.refs_1_, bf16[4,3,512,512]{3,2,1,0:T(8,128)(2,1)} %lift.1.refs_0_.refs_1_, bf16[3,128,384]{2,1,0:T(8,128)(2,1)} %copy-done.13, bf16[3,512,128]{2,1,0:T(8,128)(2,1)} %copy-done.3, bf16[3,128,384]{2,1,0:T(8,128)(2,1)} %copy-done.12, ...), custom_call_target="tpu_custom_call" | custom-call | flops 603979776 | bytes 3276800 | tf_op jit(solution)/shard_map/pallas_call | solution.py:91
  138.4 5.5 %all-to-all-start.2 = ((bf16[8,3,64,128]{3,2,1,0:T(8,128)(2,1)}), bf16[8,3,64,128]{3,2,1,0:T(8,128)(2,1)S(1)}, u32[]{:S(2)}, u32[]{:S(2)}) async-start(bf16[8,3,64,128]{3,2,1,0:T(8,128)(2,1)} %shard_map.66), calls=%async_computation.2 | async-start | bytes 786432 | tf_op jit(solution)/shard_map/all_to_all | solution.py:106
  145.9 7.4 %collective-permute-start.19 = (bf16[3,128,384]{2,1,0:T(8,128)(2,1)}, bf16[3,128,384]{2,1,0:T(8,128)(2,1)S(1)}, u32[]{:S(2)}, u32[]{:S(2)}) collective-permute-start(bf16[3,128,384]{2,1,0:T(8,128)(2,1)} %copy-done.12), channel_id=1, source_target_pairs={{0,63},{1,0},{2,1},{3,2},{4,3},{5,4},{6,5},{7,6},{8,7},{9,8},{10,9... | collective-permute-start | bytes 884744 | tf_op jit(solution)/shard_map/ppermute | solution.py:17
  156.5 5.1 %all-to-all-start.4 = ((bf16[8,2,64,128]{3,2,1,0:T(8,128)(2,1)}), bf16[8,2,64,128]{3,2,1,0:T(8,128)(2,1)S(1)}, u32[]{:S(2)}, u32[]{:S(2)}) async-start(bf16[8,2,64,128]{3,2,1,0:T(8,128)(2,1)} %shard_map.68), calls=%async_computation.4 | async-start | bytes 524288 | tf_op jit(solution)/shard_map/all_to_all | solution.py:106
  165.9 4.3 %shard_map.67 = bf16[8,3,64,128]{3,2,1,0:T(8,128)(2,1)} custom-call(bf16[4,3,512,512]{3,2,1,0:T(8,128)(2,1)} %lift.1.refs_0_.refs_1_, bf16[4,3,512,512]{3,2,1,0:T(8,128)(2,1)} %lift.1.refs_0_.refs_1_, bf16[3,256,384]{2,1,0:T(8,128)(2,1)} %copy-done.8, bf16[3,512,128]{2,1,0:T(8,128)(2,1)} %copy-done.3, bf16[3,128,384]{2,1,0:T(8,128)(2,1)} %copy-done.14, ...), custom_call_target="tpu_custom_call" | custom-call | flops 603979776 | bytes 3276800 | tf_op jit(solution)/shard_map/pallas_call | solution.py:91
  170.2 5.0 %all-to-all-start.3 = ((bf16[8,3,64,128]{3,2,1,0:T(8,128)(2,1)}), bf16[8,3,64,128]{3,2,1,0:T(8,128)(2,1)S(1)}, u32[]{:S(2)}, u32[]{:S(2)}) async-start(bf16[8,3,64,128]{3,2,1,0:T(8,128)(2,1)} %shard_map.67), calls=%async_computation.3 | async-start | bytes 786432 | tf_op jit(solution)/shard_map/all_to_all | solution.py:106
  175.3 7.6 %all-to-all-done.3 = bf16[8,3,64,128]{3,2,1,0:T(8,128)(2,1)S(1)} async-done(((bf16[8,3,64,128]{3,2,1,0:T(8,128)(2,1)}), bf16[8,3,64,128]{3,2,1,0:T(8,128)(2,1)S(1)}, u32[]{:S(2)}, u32[]{:S(2)}) %all-to-all-start.3) | async-done | bytes 393248 | tf_op jit(solution)/shard_map/all_to_all | solution.py:106
  (91 shorter events, 39.9 us)
Async XLA Ops:
  1.9 48.1 %collective-permute-start.7 = (bf16[3,512,128]{2,1,0:T(8,128)(2,1)S(1)}, bf16[3,512,128]{2,1,0:T(8,128)(2,1)S(1)}, u32[]{:S(2)}, u32[]{:S(2)}) collective-permute-start(bf16[3,512,128]{2,1,0:T(8,128)(2,1)S(1)} %fusion.2.refs_2_), channel_id=1, source_target_pairs={{0,57},{1,58},{2,59},{3,60},{4,61},{5,62},{6,63},{7,0},{8,1},{9,2}... | collective-permute-start | bytes 1179656 | tf_op jit(solution)/shard_map/ppermute | solution.py:17
  10.9 41.0 %collective-permute-start.15 = (bf16[3,256,384]{2,1,0:T(8,128)(2,1)S(1)}, bf16[3,256,384]{2,1,0:T(8,128)(2,1)}, u32[]{:S(2)}, u32[]{:S(2)}) collective-permute-start(bf16[3,256,384]{2,1,0:T(8,128)(2,1)S(1)} %fusion.refs_4_), channel_id=1, source_target_pairs={{0,57},{1,58},{2,59},{3,60},{4,61},{5,62},{6,63},{7,0},{8,1},{9,2}... | collective-permute-start | bytes 1769480 | tf_op jit(solution)/shard_map/ppermute | solution.py:17
  17.0 19.2 %collective-permute-start = (bf16[3,128,384]{2,1,0:T(8,128)(2,1)S(1)}, bf16[3,128,384]{2,1,0:T(8,128)(2,1)S(1)}, u32[]{:S(2)}, u32[]{:S(2)}) collective-permute-start(bf16[3,128,384]{2,1,0:T(8,128)(2,1)S(1)} %get-tuple-element.5.refs_1_), channel_id=1, source_target_pairs={{0,63},{1,0},{2,1},{3,2},{4,3},{5,4},{6,5},{7,6},{8,7},{9,8},{10,9... | collective-permute-start | bytes 884744 | tf_op jit(solution)/shard_map/ppermute | solution.py:17
  22.7 20.9 %collective-permute-start.2 = (bf16[3,128,384]{2,1,0:T(8,128)(2,1)S(1)}, bf16[3,128,384]{2,1,0:T(8,128)(2,1)S(1)}, u32[]{:S(2)}, u32[]{:S(2)}) collective-permute-start(bf16[3,128,384]{2,1,0:T(8,128)(2,1)S(1)} %get-tuple-element.6.refs_3_), channel_id=1, source_target_pairs={{0,63},{1,0},{2,1},{3,2},{4,3},{5,4},{6,5},{7,6},{8,7},{9,8},{10,9... | collective-permute-start | bytes 884744 | tf_op jit(solution)/shard_map/ppermute | solution.py:17
  26.9 46.1 %collective-permute-start.1 = (bf16[3,512,128]{2,1,0:T(8,128)(2,1)S(1)}, bf16[3,512,128]{2,1,0:T(8,128)(2,1)S(1)}, u32[]{:S(2)}, u32[]{:S(2)}) collective-permute-start(bf16[3,512,128]{2,1,0:T(8,128)(2,1)S(1)} %fusion.2.refs_2_), channel_id=1, source_target_pairs={{0,63},{1,0},{2,1},{3,2},{4,3},{5,4},{6,5},{7,6},{8,7},{9,8},{10,9... | collective-permute-start | bytes 1179656 | tf_op jit(solution)/shard_map/ppermute | solution.py:17
  36.3 57.6 %collective-permute-start.3 = (bf16[3,256,384]{2,1,0:T(8,128)(2,1)S(1)}, bf16[3,256,384]{2,1,0:T(8,128)(2,1)S(1)}, u32[]{:S(2)}, u32[]{:S(2)}) collective-permute-start(bf16[3,256,384]{2,1,0:T(8,128)(2,1)S(1)} %fusion.refs_4_), channel_id=1, source_target_pairs={{0,63},{1,0},{2,1},{3,2},{4,3},{5,4},{6,5},{7,6},{8,7},{9,8},{10,9... | collective-permute-start | bytes 1769480 | tf_op jit(solution)/shard_map/ppermute | solution.py:17
  43.7 36.3 %collective-permute-start.4 = (bf16[3,128,384]{2,1,0:T(8,128)(2,1)S(1)}, bf16[3,128,384]{2,1,0:T(8,128)(2,1)}, u32[]{:S(2)}, u32[]{:S(2)}) collective-permute-start(bf16[3,128,384]{2,1,0:T(8,128)(2,1)S(1)} %collective-permute-done.refs_1_), channel_id=1, source_target_pairs={{0,63},{1,0},{2,1},{3,2},{4,3},{5,4},{6,5},{7,6},{8,7},{9,8},{10,9... | collective-permute-start | bytes 884744 | tf_op jit(solution)/shard_map/ppermute | solution.py:17
  50.0 33.6 %collective-permute-start.8 = (bf16[3,512,128]{2,1,0:T(8,128)(2,1)S(1)}, bf16[3,512,128]{2,1,0:T(8,128)(2,1)}, u32[]{:S(2)}, u32[]{:S(2)}) collective-permute-start(bf16[3,512,128]{2,1,0:T(8,128)(2,1)S(1)} %collective-permute-done.7), channel_id=1, source_target_pairs={{0,1},{1,2},{2,3},{3,4},{4,5},{5,6},{6,7},{7,8},{8,9},{9,10},{10,1... | collective-permute-start | bytes 1179656 | tf_op jit(solution)/shard_map/ppermute | solution.py:17
  52.0 48.9 %collective-permute-start.16 = (bf16[3,256,384]{2,1,0:T(8,128)(2,1)}, bf16[3,256,384]{2,1,0:T(8,128)(2,1)}, u32[]{:S(2)}, u32[]{:S(2)}) collective-permute-start(bf16[3,256,384]{2,1,0:T(8,128)(2,1)} %collective-permute-done.15), channel_id=1, source_target_pairs={{0,1},{1,2},{2,3},{3,4},{4,5},{5,6},{6,7},{7,8},{8,9},{9,10},{10,1... | collective-permute-start | bytes 1769480 | tf_op jit(solution)/shard_map/ppermute | solution.py:17
  65.7 38.6 %all-to-all-start = ((bf16[8,4,64,128]{3,2,1,0:T(8,128)(2,1)}), bf16[8,4,64,128]{3,2,1,0:T(8,128)(2,1)S(1)}, u32[]{:S(2)}, u32[]{:S(2)}) async-start(bf16[8,4,64,128]{3,2,1,0:T(8,128)(2,1)} %shard_map.64), calls=%async_computation | async-start | bytes 1048576 | tf_op jit(solution)/shard_map/all_to_all | solution.py:106
  73.0 13.3 %collective-permute-start.11 = (bf16[3,128,384]{2,1,0:T(8,128)(2,1)S(1)}, bf16[3,128,384]{2,1,0:T(8,128)(2,1)}, u32[]{:S(2)}, u32[]{:S(2)}) collective-permute-start(bf16[3,128,384]{2,1,0:T(8,128)(2,1)S(1)} %collective-permute-done.2.refs_3_), channel_id=1, source_target_pairs={{0,63},{1,0},{2,1},{3,2},{4,3},{5,4},{6,5},{7,6},{8,7},{9,8},{10,9... | collective-permute-start | bytes 884744 | tf_op jit(solution)/shard_map/ppermute | solution.py:17
  80.0 19.0 %collective-permute-start.5 = (bf16[3,128,384]{2,1,0:T(8,128)(2,1)}, bf16[3,128,384]{2,1,0:T(8,128)(2,1)}, u32[]{:S(2)}, u32[]{:S(2)}) collective-permute-start(bf16[3,128,384]{2,1,0:T(8,128)(2,1)} %collective-permute-done.4), channel_id=1, source_target_pairs={{0,63},{1,0},{2,1},{3,2},{4,3},{5,4},{6,5},{7,6},{8,7},{9,8},{10,9... | collective-permute-start | bytes 884744 | tf_op jit(solution)/shard_map/ppermute | solution.py:17
  83.7 27.7 %collective-permute-start.9 = (bf16[3,512,128]{2,1,0:T(8,128)(2,1)}, bf16[3,512,128]{2,1,0:T(8,128)(2,1)S(1)}, u32[]{:S(2)}, u32[]{:S(2)}) collective-permute-start(bf16[3,512,128]{2,1,0:T(8,128)(2,1)} %collective-permute-done.8), channel_id=1, source_target_pairs={{0,1},{1,2},{2,3},{3,4},{4,5},{5,6},{6,7},{7,8},{8,9},{9,10},{10,1... | collective-permute-start | bytes 1179656 | tf_op jit(solution)/shard_map/ppermute | solution.py:17
  86.3 27.0 %collective-permute-start.12 = (bf16[3,128,384]{2,1,0:T(8,128)(2,1)}, bf16[3,128,384]{2,1,0:T(8,128)(2,1)S(1)}, u32[]{:S(2)}, u32[]{:S(2)}) collective-permute-start(bf16[3,128,384]{2,1,0:T(8,128)(2,1)} %collective-permute-done.11), channel_id=1, source_target_pairs={{0,63},{1,0},{2,1},{3,2},{4,3},{5,4},{6,5},{7,6},{8,7},{9,8},{10,9... | collective-permute-start | bytes 884744 | tf_op jit(solution)/shard_map/ppermute | solution.py:17
  99.0 21.1 %collective-permute-start.6 = (bf16[3,128,384]{2,1,0:T(8,128)(2,1)}, bf16[3,128,384]{2,1,0:T(8,128)(2,1)S(1)}, u32[]{:S(2)}, u32[]{:S(2)}) collective-permute-start(bf16[3,128,384]{2,1,0:T(8,128)(2,1)} %collective-permute-done.5), channel_id=1, source_target_pairs={{0,63},{1,0},{2,1},{3,2},{4,3},{5,4},{6,5},{7,6},{8,7},{9,8},{10,9... | collective-permute-start | bytes 884744 | tf_op jit(solution)/shard_map/ppermute | solution.py:17
  100.9 43.1 %collective-permute-start.17 = (bf16[3,256,384]{2,1,0:T(8,128)(2,1)}, bf16[3,256,384]{2,1,0:T(8,128)(2,1)S(1)}, u32[]{:S(2)}, u32[]{:S(2)}) collective-permute-start(bf16[3,256,384]{2,1,0:T(8,128)(2,1)} %collective-permute-done.16), channel_id=1, source_target_pairs={{0,1},{1,2},{2,3},{3,4},{4,5},{5,6},{6,7},{7,8},{8,9},{9,10},{10,1... | collective-permute-start | bytes 1769480 | tf_op jit(solution)/shard_map/ppermute | solution.py:17
  104.3 17.7 %all-to-all-start.1 = ((bf16[8,4,64,128]{3,2,1,0:T(8,128)(2,1)}), bf16[8,4,64,128]{3,2,1,0:T(8,128)(2,1)S(1)}, u32[]{:S(2)}, u32[]{:S(2)}) async-start(bf16[8,4,64,128]{3,2,1,0:T(8,128)(2,1)} %shard_map.65), calls=%async_computation.1 | async-start | bytes 1048576 | tf_op jit(solution)/shard_map/all_to_all | solution.py:106
  111.3 21.1 %collective-permute-start.10 = (bf16[3,512,128]{2,1,0:T(8,128)(2,1)S(1)}, bf16[3,512,128]{2,1,0:T(8,128)(2,1)S(1)}, u32[]{:S(2)}, u32[]{:S(2)}) collective-permute-start(bf16[3,512,128]{2,1,0:T(8,128)(2,1)S(1)} %collective-permute-done.9.refs_6_.refs_5_.refs_2_), channel_id=1, source_target_pairs={{0,1},{1,2},{2,3},{3,4},{4,5},{5,6},{6,7},{7,8},{8,9},{9,10},{10,1... | collective-permute-start | bytes 1179656 | tf_op jit(solution)/shard_map/ppermute | solution.py:17
  113.3 12.8 %collective-permute-start.13 = (bf16[3,128,384]{2,1,0:T(8,128)(2,1)S(1)}, bf16[3,128,384]{2,1,0:T(8,128)(2,1)S(1)}, u32[]{:S(2)}, u32[]{:S(2)}) collective-permute-start(bf16[3,128,384]{2,1,0:T(8,128)(2,1)S(1)} %collective-permute-done.12), channel_id=1, source_target_pairs={{0,63},{1,0},{2,1},{3,2},{4,3},{5,4},{6,5},{7,6},{8,7},{9,8},{10,9... | collective-permute-start | bytes 884744 | tf_op jit(solution)/shard_map/ppermute | solution.py:17
  138.4 18.1 %all-to-all-start.2 = ((bf16[8,3,64,128]{3,2,1,0:T(8,128)(2,1)}), bf16[8,3,64,128]{3,2,1,0:T(8,128)(2,1)S(1)}, u32[]{:S(2)}, u32[]{:S(2)}) async-start(bf16[8,3,64,128]{3,2,1,0:T(8,128)(2,1)} %shard_map.66), calls=%async_computation.2 | async-start | bytes 786432 | tf_op jit(solution)/shard_map/all_to_all | solution.py:106
  144.0 21.1 %collective-permute-start.18 = (bf16[3,256,384]{2,1,0:T(8,128)(2,1)S(1)}, bf16[3,256,384]{2,1,0:T(8,128)(2,1)S(1)}, u32[]{:S(2)}, u32[]{:S(2)}) collective-permute-start(bf16[3,256,384]{2,1,0:T(8,128)(2,1)S(1)} %collective-permute-done.17.refs_1_), channel_id=1, source_target_pairs={{0,1},{1,2},{2,3},{3,4},{4,5},{5,6},{6,7},{7,8},{8,9},{9,10},{10,1... | collective-permute-start | bytes 1769480 | tf_op jit(solution)/shard_map/ppermute | solution.py:17
  145.9 15.7 %collective-permute-start.19 = (bf16[3,128,384]{2,1,0:T(8,128)(2,1)}, bf16[3,128,384]{2,1,0:T(8,128)(2,1)S(1)}, u32[]{:S(2)}, u32[]{:S(2)}) collective-permute-start(bf16[3,128,384]{2,1,0:T(8,128)(2,1)} %copy-done.12), channel_id=1, source_target_pairs={{0,63},{1,0},{2,1},{3,2},{4,3},{5,4},{6,5},{7,6},{8,7},{9,8},{10,9... | collective-permute-start | bytes 884744 | tf_op jit(solution)/shard_map/ppermute | solution.py:17
  156.5 13.7 %all-to-all-start.4 = ((bf16[8,2,64,128]{3,2,1,0:T(8,128)(2,1)}), bf16[8,2,64,128]{3,2,1,0:T(8,128)(2,1)S(1)}, u32[]{:S(2)}, u32[]{:S(2)}) async-start(bf16[8,2,64,128]{3,2,1,0:T(8,128)(2,1)} %shard_map.68), calls=%async_computation.4 | async-start | bytes 524288 | tf_op jit(solution)/shard_map/all_to_all | solution.py:106
  170.2 12.7 %all-to-all-start.3 = ((bf16[8,3,64,128]{3,2,1,0:T(8,128)(2,1)}), bf16[8,3,64,128]{3,2,1,0:T(8,128)(2,1)S(1)}, u32[]{:S(2)}, u32[]{:S(2)}) async-start(bf16[8,3,64,128]{3,2,1,0:T(8,128)(2,1)} %shard_map.67), calls=%async_computation.3 | async-start | bytes 786432 | tf_op jit(solution)/shard_map/all_to_all | solution.py:106
  (18 other events, 364.2 us)
where the time goes:
time: 185 us; the launch traced here: 184 us
  starting transfers between devices  119 us (64%)
  Pallas kernels  27.9 us (15%)
  waiting for transfers between devices  26.6 us (14%)
  other arithmetic  4.97 us (3%)
  local copies, waits for them, and re-layouts  3.26 us (2%)
  between operations  1.85 us (1%)
    ppermute x20, starting transfers between devices, shifted(): lax.ppermute(shard, 'sec', [(i, (i + by) % size) for i in range(size)])  89.3 us
    all_to_all x5, starting transfers between devices, exchanged(): return lax.all_to_all(part, 'ops', 0, 0, tiled=True)  29.9 us
    pallas_call x5, Pallas kernels, finish(): pl.pallas_call(functools.partial(finish_kernel, table), grid=(1,), in_spe...  20.5 us
    ppermute x20, waiting for transfers between devices, shifted(): lax.ppermute(shard, 'sec', [(i, (i + by) % size) for i in range(size)])  19 us
    all_to_all x5, waiting for transfers between devices, exchanged(): return lax.all_to_all(part, 'ops', 0, 0, tiled=True)  7.66 us
    pallas_call x1, Pallas kernels, lift(): pl.pallas_call(lift_kernel, grid=(channels,), in_specs=[pl.BlockSpec(memo...  7.43 us
  transfers between devices with their start and end apart: 25, of which 6 were waited for; matrix products, arithmetic and copies ran while one was open for 2% of the time, Pallas kernels for 15%

commit v1 on v0

v1 whole, which is shorter than its diff:
```python
import functools

import jax
import jax.numpy as jnp
from jax import lax
from jax.experimental import pallas as pl
from jax.experimental.pallas import tpu as pltpu
from jax.sharding import PartitionSpec as P


W = 4
LANE = 128


RING = 8


def line(by):
    return lambda size: [(b + by) % size for b in range(size)]


def turned(places, by):
    return lambda size: [p - p % RING + (p + by) % RING for p in places(size)]


def moved(shard, before, after):
    size = lax.axis_size("sec")
    return lax.ppermute(shard, "sec", list(zip(before(size), after(size), strict=True)))


VMEM = pl.BlockSpec(memory_space=pltpu.VMEM)


def lift_kernel(size_ref, left_ref, vector_ref, *out_refs):
    for channel, out_ref in enumerate(out_refs):
        vector = vector_ref[0, channel]
        rows = lax.broadcasted_iota(jnp.int32, vector.shape, 0)
        vector = jnp.where(rows < size_ref[0], vector, jnp.zeros_like(vector))
        for t in range(left_ref.shape[1]):
            out_ref[t] = jnp.dot(
                left_ref[0, t, 0], vector, preferred_element_type=jnp.float32
            ).astype(jnp.bfloat16)


def lift(left_ops, wavefunction, size_left):
    channels, width = wavefunction.shape[1], wavefunction.shape[-1]
    terms = left_ops.shape[1]
    return pl.pallas_call(
        lift_kernel,
        in_specs=[pl.BlockSpec(memory_space=pltpu.SMEM), VMEM, VMEM],
        out_specs=[VMEM] * channels,
        out_shape=[jax.ShapeDtypeStruct((terms, width, width), jnp.bfloat16)] * channels,
        cost_estimate=pl.CostEstimate(
            flops=2 * channels * terms * width**3, bytes_accessed=10 * 2**20, transcendentals=0
        ),
        compiler_params=pltpu.CompilerParams(vmem_limit_bytes=16 * 2**20),
        name="lift",
    )(size_left, left_ops, wavefunction)


def finish_kernel(jobs, *refs):
    out_ref = refs[-1]
    ops, _, rows, _ = out_ref.shape
    at = 0
    for lifted, parts, columns in jobs:
        total = None
        for piece, first, lane in parts:
            deep = refs[piece].shape[2]
            for t in range(refs[piece].shape[0]):
                term = lax.dot_general(
                    refs[lifted][t, :, lane : lane + deep],
                    refs[piece][t, first : first + columns, :],
                    (((1,), (1,)), ((), ())),
                    preferred_element_type=jnp.float32,
                )
                total = term if total is None else total + term
        total = total.astype(jnp.bfloat16)
        for block in range(columns // LANE):
            out_ref[:, at] = total[:, block * LANE : (block + 1) * LANE].reshape(ops, rows, LANE)
            at += 1


def finish(lifted, jobs):
    ops, width = lax.axis_size("ops"), lifted[0].shape[-1]
    channels = sorted({job[0] for job in jobs})
    arrays = [lifted[c] for c in channels]
    place, table = {}, []
    for channel, parts, columns in jobs:
        row = []
        for piece, first, lane in parts:
            if id(piece) not in place:
                place[id(piece)] = len(arrays)
                arrays.append(piece)
            row.append((place[id(piece)], first, lane))
        table.append((channels.index(channel), row, columns))
    columns = sum(job[2] for job in jobs)
    shape = (ops, columns // LANE, width // ops, LANE)
    return pl.pallas_call(
        functools.partial(finish_kernel, table),
        in_specs=[VMEM] * len(arrays),
        out_shape=jax.ShapeDtypeStruct(shape, jnp.bfloat16),
        cost_estimate=pl.CostEstimate(
            flops=2 * columns * width * width * lifted[0].shape[0],
            bytes_accessed=2 * 2**20 + columns * 3 * 2**10,
            transcendentals=0,
        ),
        compiler_params=pltpu.CompilerParams(vmem_limit_bytes=16 * 2**20),
    )(*arrays)


def exchanged(part):
    return lax.all_to_all(part, "ops", 0, 0, tiled=True)


def summed(pieces):
    return jnp.sum(pieces.astype(jnp.float32), axis=0)


def body(wavefunction, left_ops, right_ops, size_left, size_right):
    offsets = (0, 1, W, W + 1)
    width = wavefunction.shape[-1]
    ops = lax.axis_size("ops")
    place = jnp.arange(width, dtype=jnp.int32)
    keep = place < size_right[0]

    def cut(r0, r1, c0, c1):
        inside = keep[r0:r1, None] & keep[None, c0:c1]
        return jnp.where(inside, right_ops[0, :, 0, r0:r1, c0:c1], jnp.zeros((), jnp.bfloat16))

    half, lane = width // 2, 3 * width // 4
    a = cut(0, half, 0, lane)
    right_ops, a = lax.optimization_barrier((right_ops, a))
    b0, b1 = cut(half, width, 0, lane), cut(0, width, lane, width)
    home, near, far, mid = line(0), line(-1), line(-W - 1), line(-W)
    down, up = turned(near, -2), turned(home, 2)
    a_1 = moved(a, home, near)
    n1 = moved(b1, home, near)
    b1_2 = moved(b1, home, up)
    b0_2 = moved(b0, home, up)
    a_3 = moved(a_1, near, down)
    n0 = moved(b0, home, near)
    b1_3 = moved(b1_2, up, far)
    b0_3 = moved(b0_2, up, far)
    a_4 = moved(a_3, down, mid)
    b1_4 = moved(b1_3, far, mid)
    b0_4 = moved(b0_3, far, mid)
    a_5 = moved(a_4, mid, far)

    lifted = lift(left_ops, wavefunction, size_left)

    def top(x, b):
        return [(x, 0, 0), (b, 0, lane)], half

    def low(x, b):
        return [(x, 0, 0), (b, half, lane)], half

    x0 = exchanged(finish(lifted, [(0, *top(a, b1)), (0, *low(b0, b1))]))
    x1 = exchanged(finish(lifted, [(1, *top(a_1, n1)), (1, *low(n0, n1))]))
    x2 = exchanged(finish(lifted, [(3, *low(b0_3, b1_3)), (2, *top(a_4, b1_4))]))
    x3 = exchanged(finish(lifted, [(2, *low(b0_4, b1_4)), (3, *top(a_5, b1_3))]))
    s0, s1, s2, s3 = (summed(x) for x in (x0, x1, x2, x3))
    blocks = [
        [s0[0], s0[1], s0[2], s0[3]],
        [s1[0], s1[1], s1[2], s1[3]],
        [s2[2], s2[3], s3[0], s3[1]],
        [s3[2], s3[3], s2[0], s2[1]],
    ]
    sums = jnp.stack([jnp.concatenate(row, axis=1) for row in blocks])
    rows = width // ops
    row_at = lax.axis_index("ops") * rows + jnp.arange(rows, dtype=jnp.int32)
    exists = lax.axis_index("sec") + jnp.array(offsets, jnp.int32) < lax.axis_size("sec")
    kept = (row_at < size_left[0])[None, :, None] & exists[:, None, None]
    return jnp.where(kept, sums, 0.0).astype(jnp.bfloat16)[None]


def solution(mesh):
    placed = (
        P("sec", None, None, None),
        P("ops", None, "sec", None, None),
        P("ops", None, "sec", None, None),
        P("sec"),
        P("sec"),
    )

    return jax.shard_map(
        body, mesh=mesh, in_specs=placed, out_specs=P("sec", None, "ops", None), check_vma=False
    )
```

time: 185 us -> 153 us (0.83)
  starting transfers between devices: 119 us -> 87.8 us
  Pallas kernels: 27.9 us -> 14.2 us
  other arithmetic: 4.97 us -> 11.1 us
  local copies, waits for them, and re-layouts: 3.26 us -> 7.79 us
  waiting for transfers between devices: 26.6 us -> 29.1 us
    ppermute x20 -> x12, starting transfers between devices: 89.3 us -> 48 us  [moved(): lax.ppermute(shard, 'sec', list(zip(before(size), after(size), strict=Tru...]
    pallas_call x6 -> x5, Pallas kernels: 27.9 us -> 14.2 us  [the longest x4 10.8 us: finish(): pl.pallas_call(functools.partial(finish_kernel, table), in_specs=[VMEM] *...]
    all_to_all x5 -> x4, starting transfers between devices: 29.9 us -> 39.8 us  [exchanged(): return lax.all_to_all(part, 'ops', 0, 0, tiled=True)]
    reduce_sum x5 -> x4, other arithmetic: 0.3 us -> 4.07 us  [summed(): return jnp.sum(pieces.astype(jnp.float32), axis=0)]
    unnamed x34 -> x20, local copies, waits for them, and re-layouts: 3.21 us -> 5.75 us
    all_to_all x5 -> x4, waiting for transfers between devices: 7.66 us -> 10.2 us  [exchanged(): return lax.all_to_all(part, 'ops', 0, 0, tiled=True)]
    ppermute x20 -> x12, waiting for transfers between devices: 19 us -> 19 us  [moved(): lax.ppermute(shard, 'sec', list(zip(before(size), after(size), strict=Tru...]
  transfers between devices with their start and end apart: 25 -> 16, of which waited for: 6 -> 5; matrix products, arithmetic and copies ran while one was open for 2% -> 7% of each run, Pallas kernels for 15% -> 9%
where the time goes in v1:
time: 153 us; the launch traced here: 152 us
  starting transfers between devices  87.8 us (57%)
  waiting for transfers between devices  29.1 us (19%)
  Pallas kernels  14.2 us (9%)
  other arithmetic  11.1 us (7%)
  local copies, waits for them, and re-layouts  7.79 us (5%)
  between operations  1.68 us (1%)
    ppermute x12, starting transfers between devices, moved(): lax.ppermute(shard, 'sec', list(zip(before(size), after(size), strict=Tru...  48 us
    all_to_all x4, starting transfers between devices, exchanged(): return lax.all_to_all(part, 'ops', 0, 0, tiled=True)  39.8 us
    ppermute x12, waiting for transfers between devices, moved(): lax.ppermute(shard, 'sec', list(zip(before(size), after(size), strict=Tru...  19 us
    pallas_call x4, Pallas kernels, finish(): pl.pallas_call(functools.partial(finish_kernel, table), in_specs=[VMEM] *...  10.8 us
    all_to_all x4, waiting for transfers between devices, exchanged(): return lax.all_to_all(part, 'ops', 0, 0, tiled=True)  10.2 us
    unnamed x20, local copies, waits for them, and re-layouts  5.75 us
    select_n x3, other arithmetic, cut(): jnp.where(inside, right_ops[0, :, 0, r0:r1, c0:c1], jnp.zeros((), jnp.bfl...  4.35 us
    reduce_sum x4, other arithmetic, summed(): return jnp.sum(pieces.astype(jnp.float32), axis=0)  4.07 us
  transfers between devices with their start and end apart: 16, of which 5 were waited for; matrix products, arithmetic and copies ran while one was open for 7% of the time, Pallas kernels for 9%

profile of v1, /device:TPU:1, one launch (start us, length us, event | category | flops | bytes accessed | tf_op | source)
XLA Modules:
  0.0 151.7 jit_solution(14123192570574609446)
XLA Ops:
  2.2 14.4 %collective-permute-start = (bf16[3,256,384]{2,1,0:T(8,128)(2,1)S(1)}, bf16[3,256,384]{2,1,0:T(8,128)(2,1)}, u32[]{:S(2)}, u32[]{:S(2)}) collective-permute-start(bf16[3,256,384]{2,1,0:T(8,128)(2,1)S(1)} %fusion.1.refs_1_), channel_id=1, source_target_pairs={{0,63},{1,0},{2,1},{3,2},{4,3},{5,4},{6,5},{7,6},{8,7},{9,8},{10,9... | collective-permute-start | bytes 1769480 | tf_op jit(solution)/shard_map/ppermute | solution.py:28
  16.6 2.0 %fusion.refs_3_ = bf16[3,256,384]{2,1,0:T(8,128)(2,1)} fusion(bf16[1,3,1,512,512]{4,3,1,2,0:T(8,128)(2,1)} %bitcast.60, pred[256,384]{1,0:T(8,128)(4,1)S(1)} %get-tuple-element.33), kind=kLoop, calls=%fused_computation.5 | loop fusion | flops 294912 | bytes 1277952 | tf_op jit(solution)/shard_map/jit(_where)/select_n | solution.py:128
  18.6 2.2 %collective-permute-start.2 = (bf16[3,256,384]{2,1,0:T(8,128)(2,1)}, bf16[3,256,384]{2,1,0:T(8,128)(2,1)}, u32[]{:S(2)}, u32[]{:S(2)}) collective-permute-start(bf16[3,256,384]{2,1,0:T(8,128)(2,1)} %fusion.refs_3_), channel_id=1, source_target_pairs={{0,63},{1,0},{2,1},{3,2},{4,3},{5,4},{6,5},{7,6},{8,7},{9,8},{10,9... | collective-permute-start | bytes 1769480 | tf_op jit(solution)/shard_map/ppermute | solution.py:28
  20.8 1.9 %collective-permute-start.3 = (bf16[3,256,384]{2,1,0:T(8,128)(2,1)}, bf16[3,256,384]{2,1,0:T(8,128)(2,1)}, u32[]{:S(2)}, u32[]{:S(2)}) collective-permute-start(bf16[3,256,384]{2,1,0:T(8,128)(2,1)} %fusion.refs_3_), channel_id=1, source_target_pairs={{0,2},{1,3},{2,4},{3,5},{4,6},{5,7},{6,0},{7,1},{8,10},{9,11},{10,... | collective-permute-start | bytes 1769480 | tf_op jit(solution)/shard_map/ppermute | solution.py:28
  22.9 5.7 %collective-permute-done.refs_1_ = bf16[3,256,384]{2,1,0:T(8,128)(2,1)} collective-permute-done((bf16[3,256,384]{2,1,0:T(8,128)(2,1)S(1)}, bf16[3,256,384]{2,1,0:T(8,128)(2,1)}, u32[]{:S(2)}, u32[]{:S(2)}) %collective-permute-start) | collective-permute-done | bytes 589856 | tf_op jit(solution)/shard_map/ppermute | solution.py:28
  31.5 7.5 %collective-permute-start.1 = (bf16[3,512,128]{2,1,0:T(8,128)(2,1)S(1)}, bf16[3,512,128]{2,1,0:T(8,128)(2,1)}, u32[]{:S(2)}, u32[]{:S(2)}) collective-permute-start(bf16[3,512,128]{2,1,0:T(8,128)(2,1)S(1)} %fusion.3.refs_2_), channel_id=1, source_target_pairs={{0,63},{1,0},{2,1},{3,2},{4,3},{5,4},{6,5},{7,6},{8,7},{9,8},{10,9... | collective-permute-start | bytes 1179656 | tf_op jit(solution)/shard_map/ppermute | solution.py:28
  39.1 1.9 %collective-permute-start.5 = (bf16[3,512,128]{2,1,0:T(8,128)(2,1)S(1)}, bf16[3,512,128]{2,1,0:T(8,128)(2,1)}, u32[]{:S(2)}, u32[]{:S(2)}) collective-permute-start(bf16[3,512,128]{2,1,0:T(8,128)(2,1)S(1)} %fusion.3.refs_2_), channel_id=1, source_target_pairs={{0,2},{1,3},{2,4},{3,5},{4,6},{5,7},{6,0},{7,1},{8,10},{9,11},{10,... | collective-permute-start | bytes 1179656 | tf_op jit(solution)/shard_map/ppermute | solution.py:28
  41.7 3.4 %lift.1 = (bf16[3,512,512]{2,1,0:T(8,128)(2,1)S(1)}, bf16[3,512,512]{2,1,0:T(8,128)(2,1)S(1)}, bf16[3,512,512]{2,1,0:T(8,128)(2,1)S(1)}, bf16[3,512,512]{2,1,0:T(8,128)(2,1)S(1)}) custom-call(s32[1]{0:T(128)} %copy.10.size_ref, bf16[1,3,1,512,512]{4,3,2,1,0:T(8,128)(2,1)S(1)} %copy-done.7, bf16[1,4,512,512]{3,2,1,0:T(8,128)(2,1)S(1)} %copy-done.6), custom_call_target="tpu_custom_call" | custom-call | flops 3221225472 | bytes 10485760 | tf_op jit(solution)/shard_map/lift/pallas_call | solution.py:48
  46.3 2.5 %shard_map.64 = bf16[8,4,64,128]{3,2,1,0:T(8,128)(2,1)S(1)} custom-call(bf16[3,512,512]{2,1,0:T(8,128)(2,1)S(1)} %get-tuple-element.11.refs_0_, bf16[3,256,384]{2,1,0:T(8,128)(2,1)S(1)} %fusion.1.refs_1_, bf16[3,512,128]{2,1,0:T(8,128)(2,1)S(1)} %fusion.3.refs_2_, bf16[3,256,384]{2,1,0:T(8,128)(2,1)} %fusion.refs_3_), custom_call_target="tpu_custom_call" | custom-call | flops 805306368 | bytes 3670016 | tf_op jit(solution)/shard_map/pallas_call | solution.py:98
  49.6 7.2 %all-to-all-start = ((bf16[8,4,64,128]{3,2,1,0:T(8,128)(2,1)}), bf16[8,4,64,128]{3,2,1,0:T(8,128)(2,1)}, u32[]{:S(2)}, u32[]{:S(2)}) async-start(bf16[8,4,64,128]{3,2,1,0:T(8,128)(2,1)} %copy-done), calls=%async_computation | async-start | bytes 1048576 | tf_op jit(solution)/shard_map/all_to_all | solution.py:112
  56.8 11.4 %collective-permute-done.5 = bf16[3,512,128]{2,1,0:T(8,128)(2,1)} collective-permute-done((bf16[3,512,128]{2,1,0:T(8,128)(2,1)S(1)}, bf16[3,512,128]{2,1,0:T(8,128)(2,1)}, u32[]{:S(2)}, u32[]{:S(2)}) %collective-permute-start.5) | collective-permute-done | bytes 393248 | tf_op jit(solution)/shard_map/ppermute | solution.py:28
  68.2 1.9 %collective-permute-start.6 = (bf16[3,512,128]{2,1,0:T(8,128)(2,1)}, bf16[3,512,128]{2,1,0:T(8,128)(2,1)}, u32[]{:S(2)}, u32[]{:S(2)}) collective-permute-start(bf16[3,512,128]{2,1,0:T(8,128)(2,1)} %collective-permute-done.5), channel_id=1, source_target_pairs={{2,59},{3,60},{4,61},{5,62},{6,63},{7,0},{0,1},{1,2},{10,3},{11,4}... | collective-permute-start | bytes 1179656 | tf_op jit(solution)/shard_map/ppermute | solution.py:28
  70.1 2.1 %collective-permute-start.4 = (bf16[3,256,384]{2,1,0:T(8,128)(2,1)}, bf16[3,256,384]{2,1,0:T(8,128)(2,1)}, u32[]{:S(2)}, u32[]{:S(2)}) collective-permute-start(bf16[3,256,384]{2,1,0:T(8,128)(2,1)} %collective-permute-done.3), channel_id=1, source_target_pairs={{2,59},{3,60},{4,61},{5,62},{6,63},{7,0},{0,1},{1,2},{10,3},{11,4}... | collective-permute-start | bytes 1769480 | tf_op jit(solution)/shard_map/ppermute | solution.py:28
  74.1 3.4 %collective-permute-start.8 = (bf16[3,256,384]{2,1,0:T(8,128)(2,1)}, bf16[3,256,384]{2,1,0:T(8,128)(2,1)}, u32[]{:S(2)}, u32[]{:S(2)}) collective-permute-start(bf16[3,256,384]{2,1,0:T(8,128)(2,1)} %collective-permute-done.7), channel_id=1, source_target_pairs={{61,60},{6,61},{7,62},{0,63},{1,0},{2,1},{3,2},{4,3},{5,4},{14,5},... | collective-permute-start | bytes 1769480 | tf_op jit(solution)/shard_map/ppermute | solution.py:28
  78.9 2.8 %shard_map.65 = bf16[8,4,64,128]{3,2,1,0:T(8,128)(2,1)S(1)} custom-call(bf16[3,512,512]{2,1,0:T(8,128)(2,1)S(1)} %copy-done.5, bf16[3,256,384]{2,1,0:T(8,128)(2,1)} %collective-permute-done.refs_1_, bf16[3,512,128]{2,1,0:T(8,128)(2,1)} %collective-permute-done.1.refs_2_, bf16[3,256,384]{2,1,0:T(8,128)(2,1)} %collective-permute-done.2.refs_3_), custom_call_target="tpu_custom_call" | custom-call | flops 805306368 | bytes 3670016 | tf_op jit(solution)/shard_map/pallas_call | solution.py:98
  84.4 7.5 %all-to-all-start.1 = ((bf16[8,4,64,128]{3,2,1,0:T(8,128)(2,1)}), bf16[8,4,64,128]{3,2,1,0:T(8,128)(2,1)}, u32[]{:S(2)}, u32[]{:S(2)}) async-start(bf16[8,4,64,128]{3,2,1,0:T(8,128)(2,1)} %copy-done.1), calls=%async_computation.1 | async-start | bytes 1048576 | tf_op jit(solution)/shard_map/all_to_all | solution.py:112
  94.4 2.4 %collective-permute-start.10 = (bf16[3,256,384]{2,1,0:T(8,128)(2,1)}, bf16[3,256,384]{2,1,0:T(8,128)(2,1)}, u32[]{:S(2)}, u32[]{:S(2)}) collective-permute-start(bf16[3,256,384]{2,1,0:T(8,128)(2,1)} %collective-permute-done.4.refs_2_), channel_id=1, source_target_pairs={{59,60},{60,61},{61,62},{62,63},{63,0},{0,1},{1,2},{2,3},{3,4},{4,... | collective-permute-start | bytes 1769480 | tf_op jit(solution)/shard_map/ppermute | solution.py:28
  96.8 6.5 %collective-permute-start.11 = (bf16[3,256,384]{2,1,0:T(8,128)(2,1)}, bf16[3,256,384]{2,1,0:T(8,128)(2,1)}, u32[]{:S(2)}, u32[]{:S(2)}) collective-permute-start(bf16[3,256,384]{2,1,0:T(8,128)(2,1)} %collective-permute-done.8.refs_4_), channel_id=1, source_target_pairs={{60,59},{61,60},{62,61},{63,62},{0,63},{1,0},{2,1},{3,2},{4,3},{5,... | collective-permute-start | bytes 1769480 | tf_op jit(solution)/shard_map/ppermute | solution.py:28
  103.3 2.8 %shard_map.66 = bf16[8,4,64,128]{3,2,1,0:T(8,128)(2,1)S(1)} custom-call(bf16[3,512,512]{2,1,0:T(8,128)(2,1)S(1)} %get-tuple-element.15.refs_0_, bf16[3,512,512]{2,1,0:T(8,128)(2,1)S(1)} %get-tuple-element.16.refs_1_, bf16[3,256,384]{2,1,0:T(8,128)(2,1)} %collective-permute-done.4.refs_2_, bf16[3,512,128]{2,1,0:T(8,128)(2,1)} %collective-permute-done.6.refs_3_.refs_5_, ...), custom_call_target="tpu_custom_call" | custom-call | flops 805306368 | bytes 3670016 | tf_op jit(solution)/shard_map/pallas_call | solution.py:98
  106.9 20.7 %all-to-all-start.2 = ((bf16[8,4,64,128]{3,2,1,0:T(8,128)(2,1)}), bf16[8,4,64,128]{3,2,1,0:T(8,128)(2,1)}, u32[]{:S(2)}, u32[]{:S(2)}) async-start(bf16[8,4,64,128]{3,2,1,0:T(8,128)(2,1)} %copy-done.2), calls=%async_computation.2 | async-start | bytes 1048576 | tf_op jit(solution)/shard_map/all_to_all | solution.py:112
  130.7 2.8 %shard_map.67 = bf16[8,4,64,128]{3,2,1,0:T(8,128)(2,1)S(1)} custom-call(bf16[3,512,512]{2,1,0:T(8,128)(2,1)S(1)} %get-tuple-element.15.refs_0_, bf16[3,512,512]{2,1,0:T(8,128)(2,1)S(1)} %get-tuple-element.16.refs_1_, bf16[3,256,384]{2,1,0:T(8,128)(2,1)} %collective-permute-done.10.refs_2_, bf16[3,512,128]{2,1,0:T(8,128)(2,1)S(1)} %collective-permute-done.9.refs_5_.refs_3_, ...), custom_call_target="tpu_custom_call" | custom-call | flops 805306368 | bytes 3670016 | tf_op jit(solution)/shard_map/pallas_call | solution.py:98
  134.3 2.7 %all-to-all-done.2 = bf16[8,4,64,128]{3,2,1,0:T(8,128)(2,1)} async-done(((bf16[8,4,64,128]{3,2,1,0:T(8,128)(2,1)}), bf16[8,4,64,128]{3,2,1,0:T(8,128)(2,1)}, u32[]{:S(2)}, u32[]{:S(2)}) %all-to-all-start.2) | async-done | bytes 524320 | tf_op jit(solution)/shard_map/all_to_all | solution.py:112
  137.0 4.4 %all-to-all-start.3 = ((bf16[8,4,64,128]{3,2,1,0:T(8,128)(2,1)}), bf16[8,4,64,128]{3,2,1,0:T(8,128)(2,1)S(1)}, u32[]{:S(2)}, u32[]{:S(2)}) async-start(bf16[8,4,64,128]{3,2,1,0:T(8,128)(2,1)} %copy-done.3), calls=%async_computation.3 | async-start | bytes 1048576 | tf_op jit(solution)/shard_map/all_to_all | solution.py:112
  143.4 7.4 %all-to-all-done.3 = bf16[8,4,64,128]{3,2,1,0:T(8,128)(2,1)S(1)} async-done(((bf16[8,4,64,128]{3,2,1,0:T(8,128)(2,1)}), bf16[8,4,64,128]{3,2,1,0:T(8,128)(2,1)S(1)}, u32[]{:S(2)}, u32[]{:S(2)}) %all-to-all-start.3) | async-done | bytes 524320 | tf_op jit(solution)/shard_map/all_to_all | solution.py:112
  (55 shorter events, 22.6 us)
Async XLA Ops:
  0.7 41.0 %copy-start.7 = (bf16[1,3,1,512,512]{4,3,2,1,0:T(8,128)(2,1)S(1)}, bf16[1,3,1,512,512]{4,3,2,1,0:T(8,128)(2,1)}, u32[]{:S(2)}) copy-start(bf16[1,3,1,512,512]{4,3,2,1,0:T(8,128)(2,1)} %left_ref.1) | copy-start | bytes 4718596
  0.9 40.8 %copy-start.6 = (bf16[1,4,512,512]{3,2,1,0:T(8,128)(2,1)S(1)}, bf16[1,4,512,512]{3,2,1,0:T(8,128)(2,1)}, u32[]{:S(2)}) copy-start(bf16[1,4,512,512]{3,2,1,0:T(8,128)(2,1)} %vector_ref.1) | copy-start | bytes 6291460
  2.2 26.4 %collective-permute-start = (bf16[3,256,384]{2,1,0:T(8,128)(2,1)S(1)}, bf16[3,256,384]{2,1,0:T(8,128)(2,1)}, u32[]{:S(2)}, u32[]{:S(2)}) collective-permute-start(bf16[3,256,384]{2,1,0:T(8,128)(2,1)S(1)} %fusion.1.refs_1_), channel_id=1, source_target_pairs={{0,63},{1,0},{2,1},{3,2},{4,3},{5,4},{6,5},{7,6},{8,7},{9,8},{10,9... | collective-permute-start | bytes 1769480 | tf_op jit(solution)/shard_map/ppermute | solution.py:28
  18.6 58.9 %collective-permute-start.2 = (bf16[3,256,384]{2,1,0:T(8,128)(2,1)}, bf16[3,256,384]{2,1,0:T(8,128)(2,1)}, u32[]{:S(2)}, u32[]{:S(2)}) collective-permute-start(bf16[3,256,384]{2,1,0:T(8,128)(2,1)} %fusion.refs_3_), channel_id=1, source_target_pairs={{0,63},{1,0},{2,1},{3,2},{4,3},{5,4},{6,5},{7,6},{8,7},{9,8},{10,9... | collective-permute-start | bytes 1769480 | tf_op jit(solution)/shard_map/ppermute | solution.py:28
  20.8 49.4 %collective-permute-start.3 = (bf16[3,256,384]{2,1,0:T(8,128)(2,1)}, bf16[3,256,384]{2,1,0:T(8,128)(2,1)}, u32[]{:S(2)}, u32[]{:S(2)}) collective-permute-start(bf16[3,256,384]{2,1,0:T(8,128)(2,1)} %fusion.refs_3_), channel_id=1, source_target_pairs={{0,2},{1,3},{2,4},{3,5},{4,6},{5,7},{6,0},{7,1},{8,10},{9,11},{10,... | collective-permute-start | bytes 1769480 | tf_op jit(solution)/shard_map/ppermute | solution.py:28
  28.6 45.5 %collective-permute-start.7 = (bf16[3,256,384]{2,1,0:T(8,128)(2,1)}, bf16[3,256,384]{2,1,0:T(8,128)(2,1)}, u32[]{:S(2)}, u32[]{:S(2)}) collective-permute-start(bf16[3,256,384]{2,1,0:T(8,128)(2,1)} %collective-permute-done.refs_1_), channel_id=1, source_target_pairs={{63,61},{0,6},{1,7},{2,0},{3,1},{4,2},{5,3},{6,4},{7,5},{8,14},{9,... | collective-permute-start | bytes 1769480 | tf_op jit(solution)/shard_map/ppermute | solution.py:28
  31.5 46.0 %collective-permute-start.1 = (bf16[3,512,128]{2,1,0:T(8,128)(2,1)S(1)}, bf16[3,512,128]{2,1,0:T(8,128)(2,1)}, u32[]{:S(2)}, u32[]{:S(2)}) collective-permute-start(bf16[3,512,128]{2,1,0:T(8,128)(2,1)S(1)} %fusion.3.refs_2_), channel_id=1, source_target_pairs={{0,63},{1,0},{2,1},{3,2},{4,3},{5,4},{6,5},{7,6},{8,7},{9,8},{10,9... | collective-permute-start | bytes 1179656 | tf_op jit(solution)/shard_map/ppermute | solution.py:28
  39.1 29.1 %collective-permute-start.5 = (bf16[3,512,128]{2,1,0:T(8,128)(2,1)S(1)}, bf16[3,512,128]{2,1,0:T(8,128)(2,1)}, u32[]{:S(2)}, u32[]{:S(2)}) collective-permute-start(bf16[3,512,128]{2,1,0:T(8,128)(2,1)S(1)} %fusion.3.refs_2_), channel_id=1, source_target_pairs={{0,2},{1,3},{2,4},{3,5},{4,6},{5,7},{6,0},{7,1},{8,10},{9,11},{10,... | collective-permute-start | bytes 1179656 | tf_op jit(solution)/shard_map/ppermute | solution.py:28
  45.1 1.2 copy-start.4
  46.3 31.2 %copy-start.9 = (s32[4]{0:T(128)S(1)}, s32[4]{0:T(128)}, u32[]{:S(2)}) copy-start(s32[4]{0:T(128)} %constant.18.clone) | copy-start | bytes 52
  48.8 0.8 copy-start
  49.6 34.8 %all-to-all-start = ((bf16[8,4,64,128]{3,2,1,0:T(8,128)(2,1)}), bf16[8,4,64,128]{3,2,1,0:T(8,128)(2,1)}, u32[]{:S(2)}, u32[]{:S(2)}) async-start(bf16[8,4,64,128]{3,2,1,0:T(8,128)(2,1)} %copy-done), calls=%async_computation | async-start | bytes 1048576 | tf_op jit(solution)/shard_map/all_to_all | solution.py:112
  68.2 14.3 %collective-permute-start.6 = (bf16[3,512,128]{2,1,0:T(8,128)(2,1)}, bf16[3,512,128]{2,1,0:T(8,128)(2,1)}, u32[]{:S(2)}, u32[]{:S(2)}) collective-permute-start(bf16[3,512,128]{2,1,0:T(8,128)(2,1)} %collective-permute-done.5), channel_id=1, source_target_pairs={{2,59},{3,60},{4,61},{5,62},{6,63},{7,0},{0,1},{1,2},{10,3},{11,4}... | collective-permute-start | bytes 1179656 | tf_op jit(solution)/shard_map/ppermute | solution.py:28
  70.1 24.3 %collective-permute-start.4 = (bf16[3,256,384]{2,1,0:T(8,128)(2,1)}, bf16[3,256,384]{2,1,0:T(8,128)(2,1)}, u32[]{:S(2)}, u32[]{:S(2)}) collective-permute-start(bf16[3,256,384]{2,1,0:T(8,128)(2,1)} %collective-permute-done.3), channel_id=1, source_target_pairs={{2,59},{3,60},{4,61},{5,62},{6,63},{7,0},{0,1},{1,2},{10,3},{11,4}... | collective-permute-start | bytes 1769480 | tf_op jit(solution)/shard_map/ppermute | solution.py:28
  74.1 22.7 %collective-permute-start.8 = (bf16[3,256,384]{2,1,0:T(8,128)(2,1)}, bf16[3,256,384]{2,1,0:T(8,128)(2,1)}, u32[]{:S(2)}, u32[]{:S(2)}) collective-permute-start(bf16[3,256,384]{2,1,0:T(8,128)(2,1)} %collective-permute-done.7), channel_id=1, source_target_pairs={{61,60},{6,61},{7,62},{0,63},{1,0},{2,1},{3,2},{4,3},{5,4},{14,5},... | collective-permute-start | bytes 1769480 | tf_op jit(solution)/shard_map/ppermute | solution.py:28
  77.5 1.4 copy-start.5
  82.5 20.8 %collective-permute-start.9 = (bf16[3,512,128]{2,1,0:T(8,128)(2,1)}, bf16[3,512,128]{2,1,0:T(8,128)(2,1)S(1)}, u32[]{:S(2)}, u32[]{:S(2)}) collective-permute-start(bf16[3,512,128]{2,1,0:T(8,128)(2,1)} %collective-permute-done.6.refs_3_.refs_5_), channel_id=1, source_target_pairs={{59,60},{60,61},{61,62},{62,63},{63,0},{0,1},{1,2},{2,3},{3,4},{4,... | collective-permute-start | bytes 1179656 | tf_op jit(solution)/shard_map/ppermute | solution.py:28
  84.4 22.4 %all-to-all-start.1 = ((bf16[8,4,64,128]{3,2,1,0:T(8,128)(2,1)}), bf16[8,4,64,128]{3,2,1,0:T(8,128)(2,1)}, u32[]{:S(2)}, u32[]{:S(2)}) async-start(bf16[8,4,64,128]{3,2,1,0:T(8,128)(2,1)} %copy-done.1), calls=%async_computation.1 | async-start | bytes 1048576 | tf_op jit(solution)/shard_map/all_to_all | solution.py:112
  94.4 36.3 %collective-permute-start.10 = (bf16[3,256,384]{2,1,0:T(8,128)(2,1)}, bf16[3,256,384]{2,1,0:T(8,128)(2,1)}, u32[]{:S(2)}, u32[]{:S(2)}) collective-permute-start(bf16[3,256,384]{2,1,0:T(8,128)(2,1)} %collective-permute-done.4.refs_2_), channel_id=1, source_target_pairs={{59,60},{60,61},{61,62},{62,63},{63,0},{0,1},{1,2},{2,3},{3,4},{4,... | collective-permute-start | bytes 1769480 | tf_op jit(solution)/shard_map/ppermute | solution.py:28
  96.8 33.9 %collective-permute-start.11 = (bf16[3,256,384]{2,1,0:T(8,128)(2,1)}, bf16[3,256,384]{2,1,0:T(8,128)(2,1)}, u32[]{:S(2)}, u32[]{:S(2)}) collective-permute-start(bf16[3,256,384]{2,1,0:T(8,128)(2,1)} %collective-permute-done.8.refs_4_), channel_id=1, source_target_pairs={{60,59},{61,60},{62,61},{63,62},{0,63},{1,0},{2,1},{3,2},{4,3},{5,... | collective-permute-start | bytes 1769480 | tf_op jit(solution)/shard_map/ppermute | solution.py:28
  106.9 30.2 %all-to-all-start.2 = ((bf16[8,4,64,128]{3,2,1,0:T(8,128)(2,1)}), bf16[8,4,64,128]{3,2,1,0:T(8,128)(2,1)}, u32[]{:S(2)}, u32[]{:S(2)}) async-start(bf16[8,4,64,128]{3,2,1,0:T(8,128)(2,1)} %copy-done.2), calls=%async_computation.2 | async-start | bytes 1048576 | tf_op jit(solution)/shard_map/all_to_all | solution.py:112
  133.5 0.8 copy-start.3
  134.3 16.6 %copy-start.8 = (pred[4,64]{1,0:T(4,128)(4,1)S(1)}, pred[4,64]{1,0:T(4,128)(4,1)}, u32[]{:S(2)}) copy-start(pred[4,64]{1,0:T(4,128)(4,1)} %broadcast_and_fusion.3) | copy-start | bytes 772
  137.0 13.7 %all-to-all-start.3 = ((bf16[8,4,64,128]{3,2,1,0:T(8,128)(2,1)}), bf16[8,4,64,128]{3,2,1,0:T(8,128)(2,1)S(1)}, u32[]{:S(2)}, u32[]{:S(2)}) async-start(bf16[8,4,64,128]{3,2,1,0:T(8,128)(2,1)} %copy-done.3), calls=%async_computation.3 | async-start | bytes 1048576 | tf_op jit(solution)/shard_map/all_to_all | solution.py:112
  (2 other events, 1.6 us)

commit v2 on v1

--- a/solution.py
+++ b/solution.py
@@ -53,7 +53,7 @@
         cost_estimate=pl.CostEstimate(
             flops=2 * channels * terms * width**3, bytes_accessed=10 * 2**20, transcendentals=0
         ),
-        compiler_params=pltpu.CompilerParams(vmem_limit_bytes=16 * 2**20),
+        compiler_params=pltpu.CompilerParams(vmem_limit_bytes=8 * 2**20),
         name="lift",
     )(size_left, left_ops, wavefunction)
 
@@ -104,7 +104,7 @@
             bytes_accessed=2 * 2**20 + columns * 3 * 2**10,
             transcendentals=0,
         ),
-        compiler_params=pltpu.CompilerParams(vmem_limit_bytes=16 * 2**20),
+        compiler_params=pltpu.CompilerParams(vmem_limit_bytes=8 * 2**20),
     )(*arrays)
 
 
@@ -128,9 +128,11 @@
         return jnp.where(inside, right_ops[0, :, 0, r0:r1, c0:c1], jnp.zeros((), jnp.bfloat16))
 
     half, lane = width // 2, 3 * width // 4
+    b1 = cut(0, width, lane, width)
+    right_ops, b1 = lax.optimization_barrier((right_ops, b1))
     a = cut(0, half, 0, lane)
     right_ops, a = lax.optimization_barrier((right_ops, a))
-    b0, b1 = cut(half, width, 0, lane), cut(0, width, lane, width)
+    b0 = cut(half, width, 0, lane)
     home, near, far, mid = line(0), line(-1), line(-W - 1), line(-W)
     down, up = turned(near, -2), turned(home, 2)
     a_1 = moved(a, home, near)

time: 153 us -> 150 us (0.980)
  the two profiles are of different devices: /device:TPU:1 before, /device:TPU:56 now
where the time goes in v2:
time: 150 us; the launch traced here: 149 us
  starting transfers between devices  61.8 us (41%)
  waiting for transfers between devices  52.4 us (35%)
  Pallas kernels  14.2 us (9%)
  other arithmetic  11.1 us (7%)
  local copies, waits for them, and re-layouts  7.8 us (5%)
  between operations  1.66 us (1%)
    ppermute x12, starting transfers between devices, moved(): lax.ppermute(shard, 'sec', list(zip(before(size), after(size), strict=Tru...  44.9 us
    ppermute x12, waiting for transfers between devices, moved(): lax.ppermute(shard, 'sec', list(zip(before(size), after(size), strict=Tru...  42.4 us
    all_to_all x4, starting transfers between devices, exchanged(): return lax.all_to_all(part, 'ops', 0, 0, tiled=True)  16.9 us
    pallas_call x4, Pallas kernels, finish(): pl.pallas_call(functools.partial(finish_kernel, table), in_specs=[VMEM] *...  10.8 us
    all_to_all x4, waiting for transfers between devices, exchanged(): return lax.all_to_all(part, 'ops', 0, 0, tiled=True)  9.94 us
    unnamed x20, local copies, waits for them, and re-layouts  5.76 us
    select_n x3, other arithmetic, cut(): jnp.where(inside, right_ops[0, :, 0, r0:r1, c0:c1], jnp.zeros((), jnp.bfl...  4.4 us
    reduce_sum x4, other arithmetic, summed(): return jnp.sum(pieces.astype(jnp.float32), axis=0)  4.07 us
  transfers between devices with their start and end apart: 16, of which 8 were waited for; matrix products, arithmetic and copies ran while one was open for 6% of the time, Pallas kernels for 10%

profile of v2, /device:TPU:56, one launch (start us, length us, event | category | flops | bytes accessed | tf_op | source)
XLA Modules:
  0.0 149.0 jit_solution(5119811774281838058)
XLA Ops:
  3.4 11.7 %collective-permute-start = (bf16[3,256,384]{2,1,0:T(8,128)(2,1)S(1)}, bf16[3,256,384]{2,1,0:T(8,128)(2,1)}, u32[]{:S(2)}, u32[]{:S(2)}) collective-permute-start(bf16[3,256,384]{2,1,0:T(8,128)(2,1)S(1)} %fusion.1.refs_1_), channel_id=1, source_target_pairs={{0,63},{1,0},{2,1},{3,2},{4,3},{5,4},{6,5},{7,6},{8,7},{9,8},{10,9... | collective-permute-start | bytes 1769480 | tf_op jit(solution)/shard_map/ppermute | solution.py:28
  15.2 2.0 %fusion.refs_3_ = bf16[3,256,384]{2,1,0:T(8,128)(2,1)} fusion(bf16[1,3,1,512,512]{4,3,1,2,0:T(8,128)(2,1)} %bitcast.62, pred[256,384]{1,0:T(8,128)(4,1)S(1)} %get-tuple-element.37), kind=kLoop, calls=%fused_computation.5 | loop fusion | flops 294912 | bytes 1277952 | tf_op jit(solution)/shard_map/jit(_where)/select_n | solution.py:128
  19.1 8.7 %collective-permute-done.refs_1_ = bf16[3,256,384]{2,1,0:T(8,128)(2,1)} collective-permute-done((bf16[3,256,384]{2,1,0:T(8,128)(2,1)S(1)}, bf16[3,256,384]{2,1,0:T(8,128)(2,1)}, u32[]{:S(2)}, u32[]{:S(2)}) %collective-permute-start) | collective-permute-done | bytes 589856 | tf_op jit(solution)/shard_map/ppermute | solution.py:28
  27.7 3.7 %collective-permute-start.7 = (bf16[3,256,384]{2,1,0:T(8,128)(2,1)}, bf16[3,256,384]{2,1,0:T(8,128)(2,1)}, u32[]{:S(2)}, u32[]{:S(2)}) collective-permute-start(bf16[3,256,384]{2,1,0:T(8,128)(2,1)} %collective-permute-done.refs_1_), channel_id=1, source_target_pairs={{63,61},{0,6},{1,7},{2,0},{3,1},{4,2},{5,3},{6,4},{7,5},{8,14},{9,... | collective-permute-start | bytes 1769480 | tf_op jit(solution)/shard_map/ppermute | solution.py:28
  31.4 4.8 %collective-permute-start.2 = (bf16[3,256,384]{2,1,0:T(8,128)(2,1)}, bf16[3,256,384]{2,1,0:T(8,128)(2,1)}, u32[]{:S(2)}, u32[]{:S(2)}) collective-permute-start(bf16[3,256,384]{2,1,0:T(8,128)(2,1)} %fusion.refs_3_), channel_id=1, source_target_pairs={{0,63},{1,0},{2,1},{3,2},{4,3},{5,4},{6,5},{7,6},{8,7},{9,8},{10,9... | collective-permute-start | bytes 1769480 | tf_op jit(solution)/shard_map/ppermute | solution.py:28
  36.3 1.9 %collective-permute-start.1 = (bf16[3,512,128]{2,1,0:T(8,128)(2,1)S(1)}, bf16[3,512,128]{2,1,0:T(8,128)(2,1)}, u32[]{:S(2)}, u32[]{:S(2)}) collective-permute-start(bf16[3,512,128]{2,1,0:T(8,128)(2,1)S(1)} %fusion.3.refs_2_), channel_id=1, source_target_pairs={{0,63},{1,0},{2,1},{3,2},{4,3},{5,4},{6,5},{7,6},{8,7},{9,8},{10,9... | collective-permute-start | bytes 1179656 | tf_op jit(solution)/shard_map/ppermute | solution.py:28
  38.2 5.2 %collective-permute-start.5 = (bf16[3,512,128]{2,1,0:T(8,128)(2,1)S(1)}, bf16[3,512,128]{2,1,0:T(8,128)(2,1)}, u32[]{:S(2)}, u32[]{:S(2)}) collective-permute-start(bf16[3,512,128]{2,1,0:T(8,128)(2,1)S(1)} %fusion.3.refs_2_), channel_id=1, source_target_pairs={{0,2},{1,3},{2,4},{3,5},{4,6},{5,7},{6,0},{7,1},{8,10},{9,11},{10,... | collective-permute-start | bytes 1179656 | tf_op jit(solution)/shard_map/ppermute | solution.py:28
  44.1 3.4 %lift.1 = (bf16[3,512,512]{2,1,0:T(8,128)(2,1)S(1)}, bf16[3,512,512]{2,1,0:T(8,128)(2,1)S(1)}, bf16[3,512,512]{2,1,0:T(8,128)(2,1)S(1)}, bf16[3,512,512]{2,1,0:T(8,128)(2,1)S(1)}) custom-call(s32[1]{0:T(128)} %copy.10.size_ref, bf16[1,3,1,512,512]{4,3,2,1,0:T(8,128)(2,1)S(1)} %copy-done.7, bf16[1,4,512,512]{3,2,1,0:T(8,128)(2,1)S(1)} %copy-done.6), custom_call_target="tpu_custom_call" | custom-call | flops 3221225472 | bytes 10485760 | tf_op jit(solution)/shard_map/lift/pallas_call | solution.py:48
  48.8 2.5 %shard_map.64 = bf16[8,4,64,128]{3,2,1,0:T(8,128)(2,1)S(1)} custom-call(bf16[3,512,512]{2,1,0:T(8,128)(2,1)S(1)} %get-tuple-element.13.refs_0_, bf16[3,256,384]{2,1,0:T(8,128)(2,1)S(1)} %fusion.1.refs_1_, bf16[3,512,128]{2,1,0:T(8,128)(2,1)S(1)} %fusion.3.refs_2_, bf16[3,256,384]{2,1,0:T(8,128)(2,1)} %fusion.refs_3_), custom_call_target="tpu_custom_call" | custom-call | flops 805306368 | bytes 3670016 | tf_op jit(solution)/shard_map/pallas_call | solution.py:98
  52.1 4.3 %all-to-all-start = ((bf16[8,4,64,128]{3,2,1,0:T(8,128)(2,1)}), bf16[8,4,64,128]{3,2,1,0:T(8,128)(2,1)}, u32[]{:S(2)}, u32[]{:S(2)}) async-start(bf16[8,4,64,128]{3,2,1,0:T(8,128)(2,1)} %copy-done), calls=%async_computation | async-start | bytes 1048576 | tf_op jit(solution)/shard_map/all_to_all | solution.py:112
  56.3 8.7 %collective-permute-done.5 = bf16[3,512,128]{2,1,0:T(8,128)(2,1)} collective-permute-done((bf16[3,512,128]{2,1,0:T(8,128)(2,1)S(1)}, bf16[3,512,128]{2,1,0:T(8,128)(2,1)}, u32[]{:S(2)}, u32[]{:S(2)}) %collective-permute-start.5) | collective-permute-done | bytes 393248 | tf_op jit(solution)/shard_map/ppermute | solution.py:28
  65.1 1.9 %collective-permute-start.6 = (bf16[3,512,128]{2,1,0:T(8,128)(2,1)}, bf16[3,512,128]{2,1,0:T(8,128)(2,1)}, u32[]{:S(2)}, u32[]{:S(2)}) collective-permute-start(bf16[3,512,128]{2,1,0:T(8,128)(2,1)} %collective-permute-done.5), channel_id=1, source_target_pairs={{2,59},{3,60},{4,61},{5,62},{6,63},{7,0},{0,1},{1,2},{10,3},{11,4}... | collective-permute-start | bytes 1179656 | tf_op jit(solution)/shard_map/ppermute | solution.py:28
  67.0 1.9 %collective-permute-start.4 = (bf16[3,256,384]{2,1,0:T(8,128)(2,1)}, bf16[3,256,384]{2,1,0:T(8,128)(2,1)}, u32[]{:S(2)}, u32[]{:S(2)}) collective-permute-start(bf16[3,256,384]{2,1,0:T(8,128)(2,1)} %collective-permute-done.3), channel_id=1, source_target_pairs={{2,59},{3,60},{4,61},{5,62},{6,63},{7,0},{0,1},{1,2},{10,3},{11,4}... | collective-permute-start | bytes 1769480 | tf_op jit(solution)/shard_map/ppermute | solution.py:28
  68.9 8.3 %collective-permute-done.7 = bf16[3,256,384]{2,1,0:T(8,128)(2,1)} collective-permute-done((bf16[3,256,384]{2,1,0:T(8,128)(2,1)}, bf16[3,256,384]{2,1,0:T(8,128)(2,1)}, u32[]{:S(2)}, u32[]{:S(2)}) %collective-permute-start.7) | collective-permute-done | bytes 589856 | tf_op jit(solution)/shard_map/ppermute | solution.py:28
  79.2 14.7 %collective-permute-done.1.refs_2_ = bf16[3,512,128]{2,1,0:T(8,128)(2,1)} collective-permute-done((bf16[3,512,128]{2,1,0:T(8,128)(2,1)S(1)}, bf16[3,512,128]{2,1,0:T(8,128)(2,1)}, u32[]{:S(2)}, u32[]{:S(2)}) %collective-permute-start.1) | collective-permute-done | bytes 393248 | tf_op jit(solution)/shard_map/ppermute | solution.py:28
  95.3 2.8 %shard_map.65 = bf16[8,4,64,128]{3,2,1,0:T(8,128)(2,1)S(1)} custom-call(bf16[3,512,512]{2,1,0:T(8,128)(2,1)S(1)} %copy-done.5, bf16[3,256,384]{2,1,0:T(8,128)(2,1)} %collective-permute-done.refs_1_, bf16[3,512,128]{2,1,0:T(8,128)(2,1)} %collective-permute-done.1.refs_2_, bf16[3,256,384]{2,1,0:T(8,128)(2,1)} %collective-permute-done.2.refs_3_), custom_call_target="tpu_custom_call" | custom-call | flops 805306368 | bytes 3670016 | tf_op jit(solution)/shard_map/pallas_call | solution.py:98
  100.8 4.3 %all-to-all-start.1 = ((bf16[8,4,64,128]{3,2,1,0:T(8,128)(2,1)}), bf16[8,4,64,128]{3,2,1,0:T(8,128)(2,1)}, u32[]{:S(2)}, u32[]{:S(2)}) async-start(bf16[8,4,64,128]{3,2,1,0:T(8,128)(2,1)} %copy-done.1), calls=%async_computation.1 | async-start | bytes 1048576 | tf_op jit(solution)/shard_map/all_to_all | solution.py:112
  107.5 1.9 %collective-permute-start.10 = (bf16[3,256,384]{2,1,0:T(8,128)(2,1)}, bf16[3,256,384]{2,1,0:T(8,128)(2,1)}, u32[]{:S(2)}, u32[]{:S(2)}) collective-permute-start(bf16[3,256,384]{2,1,0:T(8,128)(2,1)} %collective-permute-done.4.refs_2_), channel_id=1, source_target_pairs={{59,60},{60,61},{61,62},{62,63},{63,0},{0,1},{1,2},{2,3},{3,4},{4,... | collective-permute-start | bytes 1769480 | tf_op jit(solution)/shard_map/ppermute | solution.py:28
  109.5 6.0 %collective-permute-start.11 = (bf16[3,256,384]{2,1,0:T(8,128)(2,1)}, bf16[3,256,384]{2,1,0:T(8,128)(2,1)}, u32[]{:S(2)}, u32[]{:S(2)}) collective-permute-start(bf16[3,256,384]{2,1,0:T(8,128)(2,1)} %collective-permute-done.8.refs_4_), channel_id=1, source_target_pairs={{60,59},{61,60},{62,61},{63,62},{0,63},{1,0},{2,1},{3,2},{4,3},{5,... | collective-permute-start | bytes 1769480 | tf_op jit(solution)/shard_map/ppermute | solution.py:28
  115.5 2.8 %shard_map.66 = bf16[8,4,64,128]{3,2,1,0:T(8,128)(2,1)S(1)} custom-call(bf16[3,512,512]{2,1,0:T(8,128)(2,1)S(1)} %get-tuple-element.19.refs_0_, bf16[3,512,512]{2,1,0:T(8,128)(2,1)S(1)} %get-tuple-element.20.refs_1_, bf16[3,256,384]{2,1,0:T(8,128)(2,1)} %collective-permute-done.4.refs_2_, bf16[3,512,128]{2,1,0:T(8,128)(2,1)} %collective-permute-done.6.refs_3_.refs_5_, ...), custom_call_target="tpu_custom_call" | custom-call | flops 805306368 | bytes 3670016 | tf_op jit(solution)/shard_map/pallas_call | solution.py:98
  119.1 4.8 %all-to-all-start.2 = ((bf16[8,4,64,128]{3,2,1,0:T(8,128)(2,1)}), bf16[8,4,64,128]{3,2,1,0:T(8,128)(2,1)}, u32[]{:S(2)}, u32[]{:S(2)}) async-start(bf16[8,4,64,128]{3,2,1,0:T(8,128)(2,1)} %copy-done.2), calls=%async_computation.2 | async-start | bytes 1048576 | tf_op jit(solution)/shard_map/all_to_all | solution.py:112
  129.1 2.8 %shard_map.67 = bf16[8,4,64,128]{3,2,1,0:T(8,128)(2,1)S(1)} custom-call(bf16[3,512,512]{2,1,0:T(8,128)(2,1)S(1)} %get-tuple-element.19.refs_0_, bf16[3,512,512]{2,1,0:T(8,128)(2,1)S(1)} %get-tuple-element.20.refs_1_, bf16[3,256,384]{2,1,0:T(8,128)(2,1)} %collective-permute-done.10.refs_2_, bf16[3,512,128]{2,1,0:T(8,128)(2,1)S(1)} %collective-permute-done.9.refs_5_.refs_3_, ...), custom_call_target="tpu_custom_call" | custom-call | flops 805306368 | bytes 3670016 | tf_op jit(solution)/shard_map/pallas_call | solution.py:98
  134.3 3.5 %all-to-all-start.3 = ((bf16[8,4,64,128]{3,2,1,0:T(8,128)(2,1)}), bf16[8,4,64,128]{3,2,1,0:T(8,128)(2,1)S(1)}, u32[]{:S(2)}, u32[]{:S(2)}) async-start(bf16[8,4,64,128]{3,2,1,0:T(8,128)(2,1)} %copy-done.3), calls=%async_computation.3 | async-start | bytes 1048576 | tf_op jit(solution)/shard_map/all_to_all | solution.py:112
  139.8 8.3 %all-to-all-done.3 = bf16[8,4,64,128]{3,2,1,0:T(8,128)(2,1)S(1)} async-done(((bf16[8,4,64,128]{3,2,1,0:T(8,128)(2,1)}), bf16[8,4,64,128]{3,2,1,0:T(8,128)(2,1)S(1)}, u32[]{:S(2)}, u32[]{:S(2)}) %all-to-all-start.3) | async-done | bytes 524320 | tf_op jit(solution)/shard_map/all_to_all | solution.py:112
  (55 shorter events, 26.4 us)
Async XLA Ops:
  0.7 43.4 %copy-start.7 = (bf16[1,3,1,512,512]{4,3,2,1,0:T(8,128)(2,1)S(1)}, bf16[1,3,1,512,512]{4,3,2,1,0:T(8,128)(2,1)}, u32[]{:S(2)}) copy-start(bf16[1,3,1,512,512]{4,3,2,1,0:T(8,128)(2,1)} %left_ref.1) | copy-start | bytes 4718596
  2.0 42.1 %copy-start.6 = (bf16[1,4,512,512]{3,2,1,0:T(8,128)(2,1)S(1)}, bf16[1,4,512,512]{3,2,1,0:T(8,128)(2,1)}, u32[]{:S(2)}) copy-start(bf16[1,4,512,512]{3,2,1,0:T(8,128)(2,1)} %vector_ref.1) | copy-start | bytes 6291460
  3.4 24.3 %collective-permute-start = (bf16[3,256,384]{2,1,0:T(8,128)(2,1)S(1)}, bf16[3,256,384]{2,1,0:T(8,128)(2,1)}, u32[]{:S(2)}, u32[]{:S(2)}) collective-permute-start(bf16[3,256,384]{2,1,0:T(8,128)(2,1)S(1)} %fusion.1.refs_1_), channel_id=1, source_target_pairs={{0,63},{1,0},{2,1},{3,2},{4,3},{5,4},{6,5},{7,6},{8,7},{9,8},{10,9... | collective-permute-start | bytes 1769480 | tf_op jit(solution)/shard_map/ppermute | solution.py:28
  17.2 49.8 %collective-permute-start.3 = (bf16[3,256,384]{2,1,0:T(8,128)(2,1)}, bf16[3,256,384]{2,1,0:T(8,128)(2,1)}, u32[]{:S(2)}, u32[]{:S(2)}) collective-permute-start(bf16[3,256,384]{2,1,0:T(8,128)(2,1)} %fusion.refs_3_), channel_id=1, source_target_pairs={{0,2},{1,3},{2,4},{3,5},{4,6},{5,7},{6,0},{7,1},{8,10},{9,11},{10,... | collective-permute-start | bytes 1769480 | tf_op jit(solution)/shard_map/ppermute | solution.py:28
  27.7 49.5 %collective-permute-start.7 = (bf16[3,256,384]{2,1,0:T(8,128)(2,1)}, bf16[3,256,384]{2,1,0:T(8,128)(2,1)}, u32[]{:S(2)}, u32[]{:S(2)}) collective-permute-start(bf16[3,256,384]{2,1,0:T(8,128)(2,1)} %collective-permute-done.refs_1_), channel_id=1, source_target_pairs={{63,61},{0,6},{1,7},{2,0},{3,1},{4,2},{5,3},{6,4},{7,5},{8,14},{9,... | collective-permute-start | bytes 1769480 | tf_op jit(solution)/shard_map/ppermute | solution.py:28
  31.4 62.5 %collective-permute-start.2 = (bf16[3,256,384]{2,1,0:T(8,128)(2,1)}, bf16[3,256,384]{2,1,0:T(8,128)(2,1)}, u32[]{:S(2)}, u32[]{:S(2)}) collective-permute-start(bf16[3,256,384]{2,1,0:T(8,128)(2,1)} %fusion.refs_3_), channel_id=1, source_target_pairs={{0,63},{1,0},{2,1},{3,2},{4,3},{5,4},{6,5},{7,6},{8,7},{9,8},{10,9... | collective-permute-start | bytes 1769480 | tf_op jit(solution)/shard_map/ppermute | solution.py:28
  36.3 57.6 %collective-permute-start.1 = (bf16[3,512,128]{2,1,0:T(8,128)(2,1)S(1)}, bf16[3,512,128]{2,1,0:T(8,128)(2,1)}, u32[]{:S(2)}, u32[]{:S(2)}) collective-permute-start(bf16[3,512,128]{2,1,0:T(8,128)(2,1)S(1)} %fusion.3.refs_2_), channel_id=1, source_target_pairs={{0,63},{1,0},{2,1},{3,2},{4,3},{5,4},{6,5},{7,6},{8,7},{9,8},{10,9... | collective-permute-start | bytes 1179656 | tf_op jit(solution)/shard_map/ppermute | solution.py:28
  38.2 26.9 %collective-permute-start.5 = (bf16[3,512,128]{2,1,0:T(8,128)(2,1)S(1)}, bf16[3,512,128]{2,1,0:T(8,128)(2,1)}, u32[]{:S(2)}, u32[]{:S(2)}) collective-permute-start(bf16[3,512,128]{2,1,0:T(8,128)(2,1)S(1)} %fusion.3.refs_2_), channel_id=1, source_target_pairs={{0,2},{1,3},{2,4},{3,5},{4,6},{5,7},{6,0},{7,1},{8,10},{9,11},{10,... | collective-permute-start | bytes 1179656 | tf_op jit(solution)/shard_map/ppermute | solution.py:28
  47.6 1.2 copy-start.4
  48.8 30.4 %copy-start.9 = (s32[4]{0:T(128)S(1)}, s32[4]{0:T(128)}, u32[]{:S(2)}) copy-start(s32[4]{0:T(128)} %constant.18.clone) | copy-start | bytes 52
  51.3 0.8 copy-start
  52.1 48.8 %all-to-all-start = ((bf16[8,4,64,128]{3,2,1,0:T(8,128)(2,1)}), bf16[8,4,64,128]{3,2,1,0:T(8,128)(2,1)}, u32[]{:S(2)}, u32[]{:S(2)}) async-start(bf16[8,4,64,128]{3,2,1,0:T(8,128)(2,1)} %copy-done), calls=%async_computation | async-start | bytes 1048576 | tf_op jit(solution)/shard_map/all_to_all | solution.py:112
  65.1 33.8 %collective-permute-start.6 = (bf16[3,512,128]{2,1,0:T(8,128)(2,1)}, bf16[3,512,128]{2,1,0:T(8,128)(2,1)}, u32[]{:S(2)}, u32[]{:S(2)}) collective-permute-start(bf16[3,512,128]{2,1,0:T(8,128)(2,1)} %collective-permute-done.5), channel_id=1, source_target_pairs={{2,59},{3,60},{4,61},{5,62},{6,63},{7,0},{0,1},{1,2},{10,3},{11,4}... | collective-permute-start | bytes 1179656 | tf_op jit(solution)/shard_map/ppermute | solution.py:28
  67.0 40.5 %collective-permute-start.4 = (bf16[3,256,384]{2,1,0:T(8,128)(2,1)}, bf16[3,256,384]{2,1,0:T(8,128)(2,1)}, u32[]{:S(2)}, u32[]{:S(2)}) collective-permute-start(bf16[3,256,384]{2,1,0:T(8,128)(2,1)} %collective-permute-done.3), channel_id=1, source_target_pairs={{2,59},{3,60},{4,61},{5,62},{6,63},{7,0},{0,1},{1,2},{10,3},{11,4}... | collective-permute-start | bytes 1769480 | tf_op jit(solution)/shard_map/ppermute | solution.py:28
  77.2 32.3 %collective-permute-start.8 = (bf16[3,256,384]{2,1,0:T(8,128)(2,1)}, bf16[3,256,384]{2,1,0:T(8,128)(2,1)}, u32[]{:S(2)}, u32[]{:S(2)}) collective-permute-start(bf16[3,256,384]{2,1,0:T(8,128)(2,1)} %collective-permute-done.7), channel_id=1, source_target_pairs={{61,60},{6,61},{7,62},{0,63},{1,0},{2,1},{3,2},{4,3},{5,4},{14,5},... | collective-permute-start | bytes 1769480 | tf_op jit(solution)/shard_map/ppermute | solution.py:28
  93.9 1.4 copy-start.5
  98.9 16.6 %collective-permute-start.9 = (bf16[3,512,128]{2,1,0:T(8,128)(2,1)}, bf16[3,512,128]{2,1,0:T(8,128)(2,1)S(1)}, u32[]{:S(2)}, u32[]{:S(2)}) collective-permute-start(bf16[3,512,128]{2,1,0:T(8,128)(2,1)} %collective-permute-done.6.refs_3_.refs_5_), channel_id=1, source_target_pairs={{59,60},{60,61},{61,62},{62,63},{63,0},{0,1},{1,2},{2,3},{3,4},{4,... | collective-permute-start | bytes 1179656 | tf_op jit(solution)/shard_map/ppermute | solution.py:28
  100.8 18.3 %all-to-all-start.1 = ((bf16[8,4,64,128]{3,2,1,0:T(8,128)(2,1)}), bf16[8,4,64,128]{3,2,1,0:T(8,128)(2,1)}, u32[]{:S(2)}, u32[]{:S(2)}) async-start(bf16[8,4,64,128]{3,2,1,0:T(8,128)(2,1)} %copy-done.1), calls=%async_computation.1 | async-start | bytes 1048576 | tf_op jit(solution)/shard_map/all_to_all | solution.py:112
  107.5 20.3 %collective-permute-start.10 = (bf16[3,256,384]{2,1,0:T(8,128)(2,1)}, bf16[3,256,384]{2,1,0:T(8,128)(2,1)}, u32[]{:S(2)}, u32[]{:S(2)}) collective-permute-start(bf16[3,256,384]{2,1,0:T(8,128)(2,1)} %collective-permute-done.4.refs_2_), channel_id=1, source_target_pairs={{59,60},{60,61},{61,62},{62,63},{63,0},{0,1},{1,2},{2,3},{3,4},{4,... | collective-permute-start | bytes 1769480 | tf_op jit(solution)/shard_map/ppermute | solution.py:28
  109.5 19.6 %collective-permute-start.11 = (bf16[3,256,384]{2,1,0:T(8,128)(2,1)}, bf16[3,256,384]{2,1,0:T(8,128)(2,1)}, u32[]{:S(2)}, u32[]{:S(2)}) collective-permute-start(bf16[3,256,384]{2,1,0:T(8,128)(2,1)} %collective-permute-done.8.refs_4_), channel_id=1, source_target_pairs={{60,59},{61,60},{62,61},{63,62},{0,63},{1,0},{2,1},{3,2},{4,3},{5,... | collective-permute-start | bytes 1769480 | tf_op jit(solution)/shard_map/ppermute | solution.py:28
  119.1 15.2 %all-to-all-start.2 = ((bf16[8,4,64,128]{3,2,1,0:T(8,128)(2,1)}), bf16[8,4,64,128]{3,2,1,0:T(8,128)(2,1)}, u32[]{:S(2)}, u32[]{:S(2)}) async-start(bf16[8,4,64,128]{3,2,1,0:T(8,128)(2,1)} %copy-done.2), calls=%async_computation.2 | async-start | bytes 1048576 | tf_op jit(solution)/shard_map/all_to_all | solution.py:112
  131.8 0.8 copy-start.3
  132.6 15.5 %copy-start.8 = (pred[4,64]{1,0:T(4,128)(4,1)S(1)}, pred[4,64]{1,0:T(4,128)(4,1)}, u32[]{:S(2)}) copy-start(pred[4,64]{1,0:T(4,128)(4,1)} %broadcast_and_fusion.3) | copy-start | bytes 772
  134.3 13.7 %all-to-all-start.3 = ((bf16[8,4,64,128]{3,2,1,0:T(8,128)(2,1)}), bf16[8,4,64,128]{3,2,1,0:T(8,128)(2,1)S(1)}, u32[]{:S(2)}, u32[]{:S(2)}) async-start(bf16[8,4,64,128]{3,2,1,0:T(8,128)(2,1)} %copy-done.3), calls=%async_computation.3 | async-start | bytes 1048576 | tf_op jit(solution)/shard_map/all_to_all | solution.py:112
  (2 other events, 1.6 us)

commit v3 on v2

--- a/solution.py
+++ b/solution.py
@@ -63,17 +63,14 @@
     ops, _, rows, _ = out_ref.shape
     at = 0
     for lifted, parts, columns in jobs:
-        total = None
-        for piece, first, lane in parts:
-            deep = refs[piece].shape[2]
-            for t in range(refs[piece].shape[0]):
-                term = lax.dot_general(
-                    refs[lifted][t, :, lane : lane + deep],
-                    refs[piece][t, first : first + columns, :],
-                    (((1,), (1,)), ((), ())),
-                    preferred_element_type=jnp.float32,
-                )
-                total = term if total is None else total + term
+        terms = range(refs[lifted].shape[0])
+        rows_of = [refs[piece][t, first : first + columns, :] for t in terms for piece, first in parts]
+        total = lax.dot_general(
+            jnp.concatenate([refs[lifted][t] for t in terms], axis=1),
+            jnp.concatenate(rows_of, axis=1),
+            (((1,), (1,)), ((), ())),
+            preferred_element_type=jnp.float32,
+        )
         total = total.astype(jnp.bfloat16)
         for block in range(columns // LANE):
             out_ref[:, at] = total[:, block * LANE : (block + 1) * LANE].reshape(ops, rows, LANE)
@@ -87,11 +84,11 @@
     place, table = {}, []
     for channel, parts, columns in jobs:
         row = []
-        for piece, first, lane in parts:
+        for piece, first in parts:
             if id(piece) not in place:
                 place[id(piece)] = len(arrays)
                 arrays.append(piece)
-            row.append((place[id(piece)], first, lane))
+            row.append((place[id(piece)], first))
         table.append((channels.index(channel), row, columns))
     columns = sum(job[2] for job in jobs)
     shape = (ops, columns // LANE, width // ops, LANE)
@@ -151,10 +148,10 @@
     lifted = lift(left_ops, wavefunction, size_left)
 
     def top(x, b):
-        return [(x, 0, 0), (b, 0, lane)], half
+        return [(x, 0), (b, 0)], half
 
     def low(x, b):
-        return [(x, 0, 0), (b, half, lane)], half
+        return [(x, 0), (b, half)], half
 
     x0 = exchanged(finish(lifted, [(0, *top(a, b1)), (0, *low(b0, b1))]))
     x1 = exchanged(finish(lifted, [(1, *top(a_1, n1)), (1, *low(n0, n1))]))

time: 150 us -> 149 us (level)
  Pallas kernels: 14.2 us -> 12.6 us
    pallas_call x4, Pallas kernels: 10.8 us -> 9.18 us  [finish(): pl.pallas_call(functools.partial(finish_kernel, table), in_specs=[VMEM] *...]
  transfers between devices with their start and end apart: 16 -> 16, of which waited for: 8 -> 8; matrix products, arithmetic and copies ran while one was open for 6% -> 6% of each run, Pallas kernels for 10% -> 9%
where the time goes in v3:
time: 149 us; the launch traced here: 148 us
  starting transfers between devices  61.8 us (41%)
  waiting for transfers between devices  53.2 us (36%)
  Pallas kernels  12.6 us (8%)
  other arithmetic  11.1 us (7%)
  local copies, waits for them, and re-layouts  7.8 us (5%)
  between operations  1.66 us (1%)
    ppermute x12, starting transfers between devices, moved(): lax.ppermute(shard, 'sec', list(zip(before(size), after(size), strict=Tru...  44.9 us
    ppermute x12, waiting for transfers between devices, moved(): lax.ppermute(shard, 'sec', list(zip(before(size), after(size), strict=Tru...  43.2 us
    all_to_all x4, starting transfers between devices, exchanged(): return lax.all_to_all(part, 'ops', 0, 0, tiled=True)  16.9 us
    all_to_all x4, waiting for transfers between devices, exchanged(): return lax.all_to_all(part, 'ops', 0, 0, tiled=True)  9.94 us
    pallas_call x4, Pallas kernels, finish(): pl.pallas_call(functools.partial(finish_kernel, table), in_specs=[VMEM] *...  9.18 us
    unnamed x20, local copies, waits for them, and re-layouts  5.76 us
    select_n x3, other arithmetic, cut(): jnp.where(inside, right_ops[0, :, 0, r0:r1, c0:c1], jnp.zeros((), jnp.bfl...  4.4 us
    reduce_sum x4, other arithmetic, summed(): return jnp.sum(pieces.astype(jnp.float32), axis=0)  4.07 us
  transfers between devices with their start and end apart: 16, of which 8 were waited for; matrix products, arithmetic and copies ran while one was open for 6% of the time, Pallas kernels for 9%

profile of v3, /device:TPU:56, one launch (start us, length us, event | category | flops | bytes accessed | tf_op | source)
XLA Modules:
  0.0 148.2 jit_solution(14230714788029655683)
XLA Ops:
  3.4 11.7 %collective-permute-start = (bf16[3,256,384]{2,1,0:T(8,128)(2,1)S(1)}, bf16[3,256,384]{2,1,0:T(8,128)(2,1)}, u32[]{:S(2)}, u32[]{:S(2)}) collective-permute-start(bf16[3,256,384]{2,1,0:T(8,128)(2,1)S(1)} %fusion.1.refs_1_), channel_id=1, source_target_pairs={{0,63},{1,0},{2,1},{3,2},{4,3},{5,4},{6,5},{7,6},{8,7},{9,8},{10,9... | collective-permute-start | bytes 1769480 | tf_op jit(solution)/shard_map/ppermute | solution.py:28
  15.2 2.0 %fusion.refs_3_ = bf16[3,256,384]{2,1,0:T(8,128)(2,1)} fusion(bf16[1,3,1,512,512]{4,3,1,2,0:T(8,128)(2,1)} %bitcast.62, pred[256,384]{1,0:T(8,128)(4,1)S(1)} %get-tuple-element.37), kind=kLoop, calls=%fused_computation.5 | loop fusion | flops 294912 | bytes 1277952 | tf_op jit(solution)/shard_map/jit(_where)/select_n | solution.py:125
  19.1 8.7 %collective-permute-done.refs_1_ = bf16[3,256,384]{2,1,0:T(8,128)(2,1)} collective-permute-done((bf16[3,256,384]{2,1,0:T(8,128)(2,1)S(1)}, bf16[3,256,384]{2,1,0:T(8,128)(2,1)}, u32[]{:S(2)}, u32[]{:S(2)}) %collective-permute-start) | collective-permute-done | bytes 589856 | tf_op jit(solution)/shard_map/ppermute | solution.py:28
  27.7 3.7 %collective-permute-start.7 = (bf16[3,256,384]{2,1,0:T(8,128)(2,1)}, bf16[3,256,384]{2,1,0:T(8,128)(2,1)}, u32[]{:S(2)}, u32[]{:S(2)}) collective-permute-start(bf16[3,256,384]{2,1,0:T(8,128)(2,1)} %collective-permute-done.refs_1_), channel_id=1, source_target_pairs={{63,61},{0,6},{1,7},{2,0},{3,1},{4,2},{5,3},{6,4},{7,5},{8,14},{9,... | collective-permute-start | bytes 1769480 | tf_op jit(solution)/shard_map/ppermute | solution.py:28
  31.4 4.8 %collective-permute-start.2 = (bf16[3,256,384]{2,1,0:T(8,128)(2,1)}, bf16[3,256,384]{2,1,0:T(8,128)(2,1)}, u32[]{:S(2)}, u32[]{:S(2)}) collective-permute-start(bf16[3,256,384]{2,1,0:T(8,128)(2,1)} %fusion.refs_3_), channel_id=1, source_target_pairs={{0,63},{1,0},{2,1},{3,2},{4,3},{5,4},{6,5},{7,6},{8,7},{9,8},{10,9... | collective-permute-start | bytes 1769480 | tf_op jit(solution)/shard_map/ppermute | solution.py:28
  36.3 1.9 %collective-permute-start.1 = (bf16[3,512,128]{2,1,0:T(8,128)(2,1)S(1)}, bf16[3,512,128]{2,1,0:T(8,128)(2,1)}, u32[]{:S(2)}, u32[]{:S(2)}) collective-permute-start(bf16[3,512,128]{2,1,0:T(8,128)(2,1)S(1)} %fusion.3.refs_2_), channel_id=1, source_target_pairs={{0,63},{1,0},{2,1},{3,2},{4,3},{5,4},{6,5},{7,6},{8,7},{9,8},{10,9... | collective-permute-start | bytes 1179656 | tf_op jit(solution)/shard_map/ppermute | solution.py:28
  38.2 5.2 %collective-permute-start.5 = (bf16[3,512,128]{2,1,0:T(8,128)(2,1)S(1)}, bf16[3,512,128]{2,1,0:T(8,128)(2,1)}, u32[]{:S(2)}, u32[]{:S(2)}) collective-permute-start(bf16[3,512,128]{2,1,0:T(8,128)(2,1)S(1)} %fusion.3.refs_2_), channel_id=1, source_target_pairs={{0,2},{1,3},{2,4},{3,5},{4,6},{5,7},{6,0},{7,1},{8,10},{9,11},{10,... | collective-permute-start | bytes 1179656 | tf_op jit(solution)/shard_map/ppermute | solution.py:28
  44.1 3.4 %lift.1 = (bf16[3,512,512]{2,1,0:T(8,128)(2,1)S(1)}, bf16[3,512,512]{2,1,0:T(8,128)(2,1)S(1)}, bf16[3,512,512]{2,1,0:T(8,128)(2,1)S(1)}, bf16[3,512,512]{2,1,0:T(8,128)(2,1)S(1)}) custom-call(s32[1]{0:T(128)} %copy.10.size_ref, bf16[1,3,1,512,512]{4,3,2,1,0:T(8,128)(2,1)S(1)} %copy-done.7, bf16[1,4,512,512]{3,2,1,0:T(8,128)(2,1)S(1)} %copy-done.6), custom_call_target="tpu_custom_call" | custom-call | flops 3221225472 | bytes 10485760 | tf_op jit(solution)/shard_map/lift/pallas_call | solution.py:48
  48.8 2.1 %shard_map.64 = bf16[8,4,64,128]{3,2,1,0:T(8,128)(2,1)S(1)} custom-call(bf16[3,512,512]{2,1,0:T(8,128)(2,1)S(1)} %get-tuple-element.13.refs_0_, bf16[3,256,384]{2,1,0:T(8,128)(2,1)S(1)} %fusion.1.refs_1_, bf16[3,512,128]{2,1,0:T(8,128)(2,1)S(1)} %fusion.3.refs_2_, bf16[3,256,384]{2,1,0:T(8,128)(2,1)} %fusion.refs_3_), custom_call_target="tpu_custom_call" | custom-call | flops 805306368 | bytes 3670016 | tf_op jit(solution)/shard_map/pallas_call | solution.py:95
  51.6 4.3 %all-to-all-start = ((bf16[8,4,64,128]{3,2,1,0:T(8,128)(2,1)}), bf16[8,4,64,128]{3,2,1,0:T(8,128)(2,1)}, u32[]{:S(2)}, u32[]{:S(2)}) async-start(bf16[8,4,64,128]{3,2,1,0:T(8,128)(2,1)} %copy-done), calls=%async_computation | async-start | bytes 1048576 | tf_op jit(solution)/shard_map/all_to_all | solution.py:109
  56.0 9.1 %collective-permute-done.5 = bf16[3,512,128]{2,1,0:T(8,128)(2,1)} collective-permute-done((bf16[3,512,128]{2,1,0:T(8,128)(2,1)S(1)}, bf16[3,512,128]{2,1,0:T(8,128)(2,1)}, u32[]{:S(2)}, u32[]{:S(2)}) %collective-permute-start.5) | collective-permute-done | bytes 393248 | tf_op jit(solution)/shard_map/ppermute | solution.py:28
  65.1 1.9 %collective-permute-start.6 = (bf16[3,512,128]{2,1,0:T(8,128)(2,1)}, bf16[3,512,128]{2,1,0:T(8,128)(2,1)}, u32[]{:S(2)}, u32[]{:S(2)}) collective-permute-start(bf16[3,512,128]{2,1,0:T(8,128)(2,1)} %collective-permute-done.5), channel_id=1, source_target_pairs={{2,59},{3,60},{4,61},{5,62},{6,63},{7,0},{0,1},{1,2},{10,3},{11,4}... | collective-permute-start | bytes 1179656 | tf_op jit(solution)/shard_map/ppermute | solution.py:28
  67.0 1.9 %collective-permute-start.4 = (bf16[3,256,384]{2,1,0:T(8,128)(2,1)}, bf16[3,256,384]{2,1,0:T(8,128)(2,1)}, u32[]{:S(2)}, u32[]{:S(2)}) collective-permute-start(bf16[3,256,384]{2,1,0:T(8,128)(2,1)} %collective-permute-done.3), channel_id=1, source_target_pairs={{2,59},{3,60},{4,61},{5,62},{6,63},{7,0},{0,1},{1,2},{10,3},{11,4}... | collective-permute-start | bytes 1769480 | tf_op jit(solution)/shard_map/ppermute | solution.py:28
  68.9 8.3 %collective-permute-done.7 = bf16[3,256,384]{2,1,0:T(8,128)(2,1)} collective-permute-done((bf16[3,256,384]{2,1,0:T(8,128)(2,1)}, bf16[3,256,384]{2,1,0:T(8,128)(2,1)}, u32[]{:S(2)}, u32[]{:S(2)}) %collective-permute-start.7) | collective-permute-done | bytes 589856 | tf_op jit(solution)/shard_map/ppermute | solution.py:28
  79.2 14.7 %collective-permute-done.1.refs_2_ = bf16[3,512,128]{2,1,0:T(8,128)(2,1)} collective-permute-done((bf16[3,512,128]{2,1,0:T(8,128)(2,1)S(1)}, bf16[3,512,128]{2,1,0:T(8,128)(2,1)}, u32[]{:S(2)}, u32[]{:S(2)}) %collective-permute-start.1) | collective-permute-done | bytes 393248 | tf_op jit(solution)/shard_map/ppermute | solution.py:28
  95.3 2.4 %shard_map.65 = bf16[8,4,64,128]{3,2,1,0:T(8,128)(2,1)S(1)} custom-call(bf16[3,512,512]{2,1,0:T(8,128)(2,1)S(1)} %copy-done.5, bf16[3,256,384]{2,1,0:T(8,128)(2,1)} %collective-permute-done.refs_1_, bf16[3,512,128]{2,1,0:T(8,128)(2,1)} %collective-permute-done.1.refs_2_, bf16[3,256,384]{2,1,0:T(8,128)(2,1)} %collective-permute-done.2.refs_3_), custom_call_target="tpu_custom_call" | custom-call | flops 805306368 | bytes 3670016 | tf_op jit(solution)/shard_map/pallas_call | solution.py:95
  100.4 4.3 %all-to-all-start.1 = ((bf16[8,4,64,128]{3,2,1,0:T(8,128)(2,1)}), bf16[8,4,64,128]{3,2,1,0:T(8,128)(2,1)}, u32[]{:S(2)}, u32[]{:S(2)}) async-start(bf16[8,4,64,128]{3,2,1,0:T(8,128)(2,1)} %copy-done.1), calls=%async_computation.1 | async-start | bytes 1048576 | tf_op jit(solution)/shard_map/all_to_all | solution.py:109
  107.1 1.9 %collective-permute-start.10 = (bf16[3,256,384]{2,1,0:T(8,128)(2,1)}, bf16[3,256,384]{2,1,0:T(8,128)(2,1)}, u32[]{:S(2)}, u32[]{:S(2)}) collective-permute-start(bf16[3,256,384]{2,1,0:T(8,128)(2,1)} %collective-permute-done.4.refs_2_), channel_id=1, source_target_pairs={{59,60},{60,61},{61,62},{62,63},{63,0},{0,1},{1,2},{2,3},{3,4},{4,... | collective-permute-start | bytes 1769480 | tf_op jit(solution)/shard_map/ppermute | solution.py:28
  109.1 6.0 %collective-permute-start.11 = (bf16[3,256,384]{2,1,0:T(8,128)(2,1)}, bf16[3,256,384]{2,1,0:T(8,128)(2,1)}, u32[]{:S(2)}, u32[]{:S(2)}) collective-permute-start(bf16[3,256,384]{2,1,0:T(8,128)(2,1)} %collective-permute-done.8.refs_4_), channel_id=1, source_target_pairs={{60,59},{61,60},{62,61},{63,62},{0,63},{1,0},{2,1},{3,2},{4,3},{5,... | collective-permute-start | bytes 1769480 | tf_op jit(solution)/shard_map/ppermute | solution.py:28
  115.1 2.4 %shard_map.66 = bf16[8,4,64,128]{3,2,1,0:T(8,128)(2,1)S(1)} custom-call(bf16[3,512,512]{2,1,0:T(8,128)(2,1)S(1)} %get-tuple-element.19.refs_0_, bf16[3,512,512]{2,1,0:T(8,128)(2,1)S(1)} %get-tuple-element.20.refs_1_, bf16[3,256,384]{2,1,0:T(8,128)(2,1)} %collective-permute-done.4.refs_2_, bf16[3,512,128]{2,1,0:T(8,128)(2,1)} %collective-permute-done.6.refs_3_.refs_5_, ...), custom_call_target="tpu_custom_call" | custom-call | flops 805306368 | bytes 3670016 | tf_op jit(solution)/shard_map/pallas_call | solution.py:95
  118.3 4.8 %all-to-all-start.2 = ((bf16[8,4,64,128]{3,2,1,0:T(8,128)(2,1)}), bf16[8,4,64,128]{3,2,1,0:T(8,128)(2,1)}, u32[]{:S(2)}, u32[]{:S(2)}) async-start(bf16[8,4,64,128]{3,2,1,0:T(8,128)(2,1)} %copy-done.2), calls=%async_computation.2 | async-start | bytes 1048576 | tf_op jit(solution)/shard_map/all_to_all | solution.py:109
  128.7 2.4 %shard_map.67 = bf16[8,4,64,128]{3,2,1,0:T(8,128)(2,1)S(1)} custom-call(bf16[3,512,512]{2,1,0:T(8,128)(2,1)S(1)} %get-tuple-element.19.refs_0_, bf16[3,512,512]{2,1,0:T(8,128)(2,1)S(1)} %get-tuple-element.20.refs_1_, bf16[3,256,384]{2,1,0:T(8,128)(2,1)} %collective-permute-done.10.refs_2_, bf16[3,512,128]{2,1,0:T(8,128)(2,1)S(1)} %collective-permute-done.9.refs_5_.refs_3_, ...), custom_call_target="tpu_custom_call" | custom-call | flops 805306368 | bytes 3670016 | tf_op jit(solution)/shard_map/pallas_call | solution.py:95
  133.5 3.5 %all-to-all-start.3 = ((bf16[8,4,64,128]{3,2,1,0:T(8,128)(2,1)}), bf16[8,4,64,128]{3,2,1,0:T(8,128)(2,1)S(1)}, u32[]{:S(2)}, u32[]{:S(2)}) async-start(bf16[8,4,64,128]{3,2,1,0:T(8,128)(2,1)} %copy-done.3), calls=%async_computation.3 | async-start | bytes 1048576 | tf_op jit(solution)/shard_map/all_to_all | solution.py:109
  139.0 8.3 %all-to-all-done.3 = bf16[8,4,64,128]{3,2,1,0:T(8,128)(2,1)S(1)} async-done(((bf16[8,4,64,128]{3,2,1,0:T(8,128)(2,1)}), bf16[8,4,64,128]{3,2,1,0:T(8,128)(2,1)S(1)}, u32[]{:S(2)}, u32[]{:S(2)}) %all-to-all-start.3) | async-done | bytes 524320 | tf_op jit(solution)/shard_map/all_to_all | solution.py:109
  (55 shorter events, 26.8 us)
Async XLA Ops:
  0.7 43.4 %copy-start.7 = (bf16[1,3,1,512,512]{4,3,2,1,0:T(8,128)(2,1)S(1)}, bf16[1,3,1,512,512]{4,3,2,1,0:T(8,128)(2,1)}, u32[]{:S(2)}) copy-start(bf16[1,3,1,512,512]{4,3,2,1,0:T(8,128)(2,1)} %left_ref.1) | copy-start | bytes 4718596
  2.0 42.1 %copy-start.6 = (bf16[1,4,512,512]{3,2,1,0:T(8,128)(2,1)S(1)}, bf16[1,4,512,512]{3,2,1,0:T(8,128)(2,1)}, u32[]{:S(2)}) copy-start(bf16[1,4,512,512]{3,2,1,0:T(8,128)(2,1)} %vector_ref.1) | copy-start | bytes 6291460
  3.4 24.3 %collective-permute-start = (bf16[3,256,384]{2,1,0:T(8,128)(2,1)S(1)}, bf16[3,256,384]{2,1,0:T(8,128)(2,1)}, u32[]{:S(2)}, u32[]{:S(2)}) collective-permute-start(bf16[3,256,384]{2,1,0:T(8,128)(2,1)S(1)} %fusion.1.refs_1_), channel_id=1, source_target_pairs={{0,63},{1,0},{2,1},{3,2},{4,3},{5,4},{6,5},{7,6},{8,7},{9,8},{10,9... | collective-permute-start | bytes 1769480 | tf_op jit(solution)/shard_map/ppermute | solution.py:28
  17.2 49.8 %collective-permute-start.3 = (bf16[3,256,384]{2,1,0:T(8,128)(2,1)}, bf16[3,256,384]{2,1,0:T(8,128)(2,1)}, u32[]{:S(2)}, u32[]{:S(2)}) collective-permute-start(bf16[3,256,384]{2,1,0:T(8,128)(2,1)} %fusion.refs_3_), channel_id=1, source_target_pairs={{0,2},{1,3},{2,4},{3,5},{4,6},{5,7},{6,0},{7,1},{8,10},{9,11},{10,... | collective-permute-start | bytes 1769480 | tf_op jit(solution)/shard_map/ppermute | solution.py:28
  27.7 49.5 %collective-permute-start.7 = (bf16[3,256,384]{2,1,0:T(8,128)(2,1)}, bf16[3,256,384]{2,1,0:T(8,128)(2,1)}, u32[]{:S(2)}, u32[]{:S(2)}) collective-permute-start(bf16[3,256,384]{2,1,0:T(8,128)(2,1)} %collective-permute-done.refs_1_), channel_id=1, source_target_pairs={{63,61},{0,6},{1,7},{2,0},{3,1},{4,2},{5,3},{6,4},{7,5},{8,14},{9,... | collective-permute-start | bytes 1769480 | tf_op jit(solution)/shard_map/ppermute | solution.py:28
  31.4 62.5 %collective-permute-start.2 = (bf16[3,256,384]{2,1,0:T(8,128)(2,1)}, bf16[3,256,384]{2,1,0:T(8,128)(2,1)}, u32[]{:S(2)}, u32[]{:S(2)}) collective-permute-start(bf16[3,256,384]{2,1,0:T(8,128)(2,1)} %fusion.refs_3_), channel_id=1, source_target_pairs={{0,63},{1,0},{2,1},{3,2},{4,3},{5,4},{6,5},{7,6},{8,7},{9,8},{10,9... | collective-permute-start | bytes 1769480 | tf_op jit(solution)/shard_map/ppermute | solution.py:28
  36.3 57.6 %collective-permute-start.1 = (bf16[3,512,128]{2,1,0:T(8,128)(2,1)S(1)}, bf16[3,512,128]{2,1,0:T(8,128)(2,1)}, u32[]{:S(2)}, u32[]{:S(2)}) collective-permute-start(bf16[3,512,128]{2,1,0:T(8,128)(2,1)S(1)} %fusion.3.refs_2_), channel_id=1, source_target_pairs={{0,63},{1,0},{2,1},{3,2},{4,3},{5,4},{6,5},{7,6},{8,7},{9,8},{10,9... | collective-permute-start | bytes 1179656 | tf_op jit(solution)/shard_map/ppermute | solution.py:28
  38.2 26.9 %collective-permute-start.5 = (bf16[3,512,128]{2,1,0:T(8,128)(2,1)S(1)}, bf16[3,512,128]{2,1,0:T(8,128)(2,1)}, u32[]{:S(2)}, u32[]{:S(2)}) collective-permute-start(bf16[3,512,128]{2,1,0:T(8,128)(2,1)S(1)} %fusion.3.refs_2_), channel_id=1, source_target_pairs={{0,2},{1,3},{2,4},{3,5},{4,6},{5,7},{6,0},{7,1},{8,10},{9,11},{10,... | collective-permute-start | bytes 1179656 | tf_op jit(solution)/shard_map/ppermute | solution.py:28
  47.6 1.2 copy-start.4
  48.8 30.4 %copy-start.9 = (s32[4]{0:T(128)S(1)}, s32[4]{0:T(128)}, u32[]{:S(2)}) copy-start(s32[4]{0:T(128)} %constant.18.clone) | copy-start | bytes 52
  50.9 0.8 copy-start
  51.6 48.8 %all-to-all-start = ((bf16[8,4,64,128]{3,2,1,0:T(8,128)(2,1)}), bf16[8,4,64,128]{3,2,1,0:T(8,128)(2,1)}, u32[]{:S(2)}, u32[]{:S(2)}) async-start(bf16[8,4,64,128]{3,2,1,0:T(8,128)(2,1)} %copy-done), calls=%async_computation | async-start | bytes 1048576 | tf_op jit(solution)/shard_map/all_to_all | solution.py:109
  65.1 33.4 %collective-permute-start.6 = (bf16[3,512,128]{2,1,0:T(8,128)(2,1)}, bf16[3,512,128]{2,1,0:T(8,128)(2,1)}, u32[]{:S(2)}, u32[]{:S(2)}) collective-permute-start(bf16[3,512,128]{2,1,0:T(8,128)(2,1)} %collective-permute-done.5), channel_id=1, source_target_pairs={{2,59},{3,60},{4,61},{5,62},{6,63},{7,0},{0,1},{1,2},{10,3},{11,4}... | collective-permute-start | bytes 1179656 | tf_op jit(solution)/shard_map/ppermute | solution.py:28
  67.0 40.1 %collective-permute-start.4 = (bf16[3,256,384]{2,1,0:T(8,128)(2,1)}, bf16[3,256,384]{2,1,0:T(8,128)(2,1)}, u32[]{:S(2)}, u32[]{:S(2)}) collective-permute-start(bf16[3,256,384]{2,1,0:T(8,128)(2,1)} %collective-permute-done.3), channel_id=1, source_target_pairs={{2,59},{3,60},{4,61},{5,62},{6,63},{7,0},{0,1},{1,2},{10,3},{11,4}... | collective-permute-start | bytes 1769480 | tf_op jit(solution)/shard_map/ppermute | solution.py:28
  77.2 31.9 %collective-permute-start.8 = (bf16[3,256,384]{2,1,0:T(8,128)(2,1)}, bf16[3,256,384]{2,1,0:T(8,128)(2,1)}, u32[]{:S(2)}, u32[]{:S(2)}) collective-permute-start(bf16[3,256,384]{2,1,0:T(8,128)(2,1)} %collective-permute-done.7), channel_id=1, source_target_pairs={{61,60},{6,61},{7,62},{0,63},{1,0},{2,1},{3,2},{4,3},{5,4},{14,5},... | collective-permute-start | bytes 1769480 | tf_op jit(solution)/shard_map/ppermute | solution.py:28
  93.9 1.4 copy-start.5
  98.5 16.6 %collective-permute-start.9 = (bf16[3,512,128]{2,1,0:T(8,128)(2,1)}, bf16[3,512,128]{2,1,0:T(8,128)(2,1)S(1)}, u32[]{:S(2)}, u32[]{:S(2)}) collective-permute-start(bf16[3,512,128]{2,1,0:T(8,128)(2,1)} %collective-permute-done.6.refs_3_.refs_5_), channel_id=1, source_target_pairs={{59,60},{60,61},{61,62},{62,63},{63,0},{0,1},{1,2},{2,3},{3,4},{4,... | collective-permute-start | bytes 1179656 | tf_op jit(solution)/shard_map/ppermute | solution.py:28
  100.4 17.9 %all-to-all-start.1 = ((bf16[8,4,64,128]{3,2,1,0:T(8,128)(2,1)}), bf16[8,4,64,128]{3,2,1,0:T(8,128)(2,1)}, u32[]{:S(2)}, u32[]{:S(2)}) async-start(bf16[8,4,64,128]{3,2,1,0:T(8,128)(2,1)} %copy-done.1), calls=%async_computation.1 | async-start | bytes 1048576 | tf_op jit(solution)/shard_map/all_to_all | solution.py:109
  107.1 20.3 %collective-permute-start.10 = (bf16[3,256,384]{2,1,0:T(8,128)(2,1)}, bf16[3,256,384]{2,1,0:T(8,128)(2,1)}, u32[]{:S(2)}, u32[]{:S(2)}) collective-permute-start(bf16[3,256,384]{2,1,0:T(8,128)(2,1)} %collective-permute-done.4.refs_2_), channel_id=1, source_target_pairs={{59,60},{60,61},{61,62},{62,63},{63,0},{0,1},{1,2},{2,3},{3,4},{4,... | collective-permute-start | bytes 1769480 | tf_op jit(solution)/shard_map/ppermute | solution.py:28
  109.1 19.6 %collective-permute-start.11 = (bf16[3,256,384]{2,1,0:T(8,128)(2,1)}, bf16[3,256,384]{2,1,0:T(8,128)(2,1)}, u32[]{:S(2)}, u32[]{:S(2)}) collective-permute-start(bf16[3,256,384]{2,1,0:T(8,128)(2,1)} %collective-permute-done.8.refs_4_), channel_id=1, source_target_pairs={{60,59},{61,60},{62,61},{63,62},{0,63},{1,0},{2,1},{3,2},{4,3},{5,... | collective-permute-start | bytes 1769480 | tf_op jit(solution)/shard_map/ppermute | solution.py:28
  118.3 15.2 %all-to-all-start.2 = ((bf16[8,4,64,128]{3,2,1,0:T(8,128)(2,1)}), bf16[8,4,64,128]{3,2,1,0:T(8,128)(2,1)}, u32[]{:S(2)}, u32[]{:S(2)}) async-start(bf16[8,4,64,128]{3,2,1,0:T(8,128)(2,1)} %copy-done.2), calls=%async_computation.2 | async-start | bytes 1048576 | tf_op jit(solution)/shard_map/all_to_all | solution.py:109
  131.0 0.8 copy-start.3
  131.8 15.5 %copy-start.8 = (pred[4,64]{1,0:T(4,128)(4,1)S(1)}, pred[4,64]{1,0:T(4,128)(4,1)}, u32[]{:S(2)}) copy-start(pred[4,64]{1,0:T(4,128)(4,1)} %broadcast_and_fusion.3) | copy-start | bytes 772
  133.5 13.7 %all-to-all-start.3 = ((bf16[8,4,64,128]{3,2,1,0:T(8,128)(2,1)}), bf16[8,4,64,128]{3,2,1,0:T(8,128)(2,1)S(1)}, u32[]{:S(2)}, u32[]{:S(2)}) async-start(bf16[8,4,64,128]{3,2,1,0:T(8,128)(2,1)} %copy-done.3), calls=%async_computation.3 | async-start | bytes 1048576 | tf_op jit(solution)/shard_map/all_to_all | solution.py:109
  (2 other events, 1.6 us)
